TPU v7x, 32 devices: a whole 2x2x4 slice. The times are simulated.
32 devices in a mesh: row: 8 (over z, x), col: 4 (over y, core).
Axes of the slice: x: 2, y: 2, z: 4, core: 2. Of those that a mesh axis runs over, the one named last changes fastest.
Arguments:
- trailing: float32 [8192, 1536], P('row', 'col'), may hold values from -6 to 6
- reflectors: float32 [8192, 256], P('row', 'col'), may hold values from -6 to 6
- factor: float32 [256, 256], replicated, as said below
- column_sums: float32 [8192, 8], P('row', 'col'), may hold values from -6 to 6
- row_sums: float32 [16, 1536], P('row', 'col'), may hold values from -6 to 6
Outputs:
- updated: float32 [8192, 1536], P('row', 'col')
- column_checks: float32 [8192, 8], P('row', 'col')
- row_checks: float32 [16, 1536], P('row', 'col')
Inputs may be any that keep to these rules, and one draw needn't show every extreme that they name: `factor`: zero below the diagonal.
All inputs are finite; a program needn't handle non-finite values.
Results may differ from a plain program's by a relative error of at most 0.000067.
Values sent between devices are 32-bit elements; how exact they have to be, the bound alone decides.
No kernel may reach another device: no remote copies, remote signals or barrier semaphores. Data moves between devices by JAX's collectives and lax.ppermute only.
A program may use at most 64 MiB of HBM per device.

v0:
```python
import jax
import jax.numpy as jnp
from jax import lax
from jax.sharding import PartitionSpec as P


def matmul(left, right):
    return jnp.dot(left, right, precision=lax.Precision.HIGHEST, preferred_element_type=jnp.float32)


def shards(trailing, reflectors, factor, column_sums, row_sums):
    panel = lax.all_gather(reflectors, "col", axis=1, tiled=True)
    columns = trailing.shape[1]
    joined = jnp.concatenate([trailing, column_sums], axis=1)
    product = matmul(panel.T, joined)
    product_main = product[:, :columns]
    product_check = product[:, columns:]
    summed_main, summed_check = lax.psum((product_main, product_check), "row")
    main_image = matmul(factor.T, summed_main)
    check_image = matmul(factor.T, summed_check)
    updated = trailing - matmul(panel, main_image)
    column_checks = column_sums - matmul(panel, check_image)
    count = trailing.shape[0]
    local = jnp.arange(count).astype(jnp.float32)
    scale = 1.0 / jnp.sqrt(jnp.float32(count))
    weights = jnp.stack([jnp.ones((count,), jnp.float32) * scale, (local + 1.0) * scale / count])
    check_coeff = matmul(weights, panel)
    row_checks = row_sums - matmul(check_coeff, main_image)
    return (updated, column_checks, row_checks)


def solution(mesh):
    placed = (P("row", "col"), P("row", "col"), P(), P("row", "col"), P("row", "col"))
    return jax.shard_map(
        shards,
        mesh=mesh,
        in_specs=placed,
        out_specs=(P("row", "col"), P("row", "col"), P("row", "col")),
        check_vma=False,
    )
```

profile of v0, /device:TPU:0, one launch (start us, length us, event | category | flops | bytes accessed | tf_op | source)
XLA Modules:
  0.0 139.2 jit_solution(17977182560160107712)
XLA Ops:
  7.2 0.0 copy-start
  7.2 0.0 all-gather.2.cloned.1.call-start
  7.2 0.7 all-gather.2.cloned.1.call-update
  7.9 0.0 all-reduce.3.cloned.1.call-start
  8.0 0.9 copy.8
  8.9 0.0 copy-start.2
  8.9 3.1 %copy.9 = f32[1024,384]{0,1:T(8,128)} copy(f32[1024,384]{1,0:T(8,128)} %param.5) | data formatting | bytes 3145728 | tf_op args[0]
  12.0 17.0 %all-gather.2.cloned.1.call-done = f32[1024,256]{0,1:T(8,128)} async-done(((f32[1024,64]{0,1:T(8,128)}), f32[1024,256]{0,1:T(8,128)}) %all-gather.2.cloned.1.call-update) | async-done | bytes 1048592 | tf_op jit(solution)/shard_map/all_gather | solution.py:12
  29.0 0.0 copy-done.2
  29.0 0.0 copy-start.1
  29.0 4.7 %fusion.4 = f32[256,386]{0,1:T(8,128)S(1)} fusion(f32[1024,256]{0,1:T(8,128)} %all-gather.2.cloned.1.call-done, f32[1024,2]{1,0:T(8,128)S(1)} %copy.8, f32[1024,384]{1,0:T(8,128)S(1)} %copy-done.2), kind=kOutput, calls=%fused_computation.5 | convolution fusion | flops 1214646272 | bytes 3024896 | tf_op jit(solution)/shard_map/dot_general | solution.py:8
  33.8 0.0 copy-start.4
  33.8 0.8 slice.8
  34.5 21.3 %psum.15 = f32[256,2]{0,1:T(2,128)S(1)} all-reduce(f32[256,2]{0,1:T(2,128)S(1)} %slice.9), channel_id=1, replica_groups=mesh['row'=8,'col'=4] {'row'}, use_global_device_ids=true, to_apply=%region_1.0 | all-reduce | flops 512 | bytes 4096 | tf_op jit(solution)/shard_map/psum | solution.py:18
  55.9 0.0 all-reduce.3.cloned.1.call-update
  55.9 0.0 copy-done.1
  55.9 0.0 copy-start.3
  55.9 0.9 fusion.8
  56.8 0.0 copy-done
  56.8 0.2 fusion.13
  57.0 0.0 copy-done.4
  57.1 1.2 fusion.7
  58.3 65.9 %all-reduce.3.cloned.1.call-done = f32[256,384]{0,1:T(8,128)} async-done(((f32[256,384]{0,1:T(8,128)}), f32[256,384]{0,1:T(8,128)}) %all-reduce.3.cloned.1.call-update) | async-done | bytes 393232 | tf_op jit(solution)/shard_map/psum | solution.py:18
  124.2 1.5 %fusion.12 = f32[384,256]{1,0:T(8,128)S(1)} fusion(f32[256,384]{0,1:T(8,128)} %all-reduce.3.cloned.1.call-done, f32[256,256]{1,0:T(8,128)S(1)} %copy-done), kind=kOutput, calls=%fused_computation.14 | convolution fusion | flops 301989888 | bytes 1048576 | tf_op jit(solution)/shard_map/dot_general | solution.py:8
  125.7 0.0 copy-done.3
  125.7 2.6 %bitcast_subtract_fusion = f32[1024,384]{0,1:T(8,128)} fusion(f32[1024,384]{0,1:T(8,128)S(1)} %copy-done.3, f32[384,256]{1,0:T(8,128)S(1)} %fusion.12, f32[1024,256]{0,1:T(8,128)S(1)} %copy-done.1), kind=kOutput, calls=%fused_computation.4 | convolution fusion | flops 1208352768 | bytes 4587520 | tf_op jit(solution)/shard_map/dot_general | solution.py:8
  128.3 0.0 copy-start.5
  128.3 3.0 %copy.10 = f32[1024,384]{1,0:T(8,128)} copy(f32[1024,384]{0,1:T(8,128)} %bitcast_subtract_fusion) | data formatting | bytes 3145728
  131.4 0.0 copy-done.5
  131.4 1.0 convolution_subtract_fusion
  (2 shorter events, 0.0 us)
Async XLA Ops:
  7.2 49.7 %copy-start = (f32[256,256]{1,0:T(8,128)S(1)}, f32[256,256]{1,0:T(8,128)}, u32[]{:S(2)}) copy-start(f32[256,256]{1,0:T(8,128)} %param.7) | copy-start | bytes 786436
  7.2 21.8 %all-gather.2.cloned.1.call-start = ((), (), s32[]{:S(2)}) async-start(), calls=%async_computation | async-start | bytes 1310720 | tf_op jit(solution)/shard_map/all_gather | solution.py:12
  7.9 116.3 %all-reduce.3.cloned.1.call-start = ((), (), s32[]{:S(2)}) async-start(), calls=%async_computation.1 | async-start | bytes 786432 | tf_op jit(solution)/shard_map/psum | solution.py:18
  8.9 20.1 %copy-start.2 = (f32[1024,384]{1,0:T(8,128)S(1)}, f32[1024,384]{1,0:T(8,128)}, u32[]{:S(2)}) copy-start(f32[1024,384]{1,0:T(8,128)} %param.5) | copy-start | bytes 4718596
  29.0 26.9 %copy-start.1 = (f32[1024,256]{0,1:T(8,128)S(1)}, f32[1024,256]{0,1:T(8,128)}, u32[]{:S(2)}) copy-start(f32[1024,256]{0,1:T(8,128)} %all-gather.2.cloned.1.call-done) | copy-start | bytes 3145732
  33.8 23.3 %copy-start.4 = (f32[1024,2]{0,1:T(2,128)S(1)}, f32[1024,2]{0,1:T(2,128)}, u32[]{:S(2)}) copy-start(f32[1024,2]{0,1:T(2,128)} %param.8) | copy-start | bytes 24580
  55.9 69.8 %copy-start.3 = (f32[1024,384]{0,1:T(8,128)S(1)}, f32[1024,384]{0,1:T(8,128)}, u32[]{:S(2)}) copy-start(f32[1024,384]{0,1:T(8,128)} %copy.9) | copy-start | bytes 4718596
  128.3 3.0 %copy-start.5 = (f32[2,384]{1,0:T(2,128)S(1)}, f32[2,384]{1,0:T(2,128)}, u32[]{:S(2)}) copy-start(f32[2,384]{1,0:T(2,128)} %param.9) | copy-start | bytes 9220
Sparse Core Ops, SparseCore 0:
  9.5 19.4 all-gather.1
  56.0 68.1 all-reduce.2
where the time goes:
time: 139 us
  waiting for transfers between devices  83.6 us (60%)
  blocking collectives  21.3 us (15%)
  between operations  14.1 us (10%)
  matrix products  12.2 us (9%)
  local copies, waits for them, and re-layouts  7.89 us (6%)
    psum x1, waiting for transfers between devices, shards(): summed_main, summed_check = lax.psum((product_main, product_check), 'row')  65.9 us
    psum x1, blocking collectives, shards(): summed_main, summed_check = lax.psum((product_main, product_check), 'row')  21.3 us
    all_gather x1, waiting for transfers between devices, shards(): panel = lax.all_gather(reflectors, 'col', axis=1, tiled=True)  17 us
    dot_general x7, matrix products, matmul(): jnp.dot(left, right, precision=lax.Precision.HIGHEST, preferred_element_t...  12.2 us
    unnamed x15, local copies, waits for them, and re-layouts  7.12 us
  transfers between devices with their start and end apart: 2, of which 2 were waited for; matrix products, arithmetic and copies ran while one was open for 5% of the time, Pallas kernels for 0%

commit v1 on v0

v1 whole, which is shorter than its diff:
```python
import jax
import jax.numpy as jnp
from jax import lax
from jax.sharding import PartitionSpec as P

EXTRA = 8


def dot(left, right, dims=((1,), (0,))):
    return lax.dot_general(left, right, (dims, ((), ())), precision=lax.Precision.HIGH, preferred_element_type=jnp.float32)


def swap(value, axis, size, distance):
    return lax.ppermute(value, axis, [(i, i ^ distance) for i in range(size)])


def xor_blocks(value, dim, blocks, index):
    shape = value.shape
    width = shape[dim] // blocks
    step = 1
    while step < blocks:
        split = shape[:dim] + (blocks // (2 * step), 2, step * width) + shape[dim + 1 :]
        turned = jnp.flip(value.reshape(split), dim + 1).reshape(shape)
        value = jnp.where((index // step) % 2 == 1, turned, value)
        step *= 2
    return value


def check_weights(count):
    local = jnp.arange(count).astype(jnp.float32)
    scale = 1.0 / jnp.sqrt(jnp.float32(count))
    return jnp.stack([jnp.ones((count,), jnp.float32) * scale, (local + 1.0) * scale / count])


def plain(trailing, reflectors, factor, column_sums, row_sums):
    panel = lax.all_gather(reflectors, "col", axis=1, tiled=True)
    columns = trailing.shape[1]
    joined = jnp.concatenate([trailing, column_sums], axis=1)
    image = dot(factor.T, lax.psum(dot(panel.T, joined), "row"))
    joined = joined - dot(panel, image)
    coeff = dot(check_weights(trailing.shape[0]), panel)
    return (joined[:, :columns], joined[:, columns:], row_sums - dot(coeff, image[:, :columns]))


def steps(n_row, n_col, trailing, reflectors, factor, column_sums, row_sums):
    rows, columns = trailing.shape
    width = reflectors.shape[1]
    row = lax.axis_index("row")
    col = lax.axis_index("col")
    side = row % 2
    half = n_col // 4 * width
    sums = column_sums.T
    order = sorted(range(1, n_col), key=lambda s: (s & (s - 1), -s))
    got = {0: reflectors.T}
    for s in order:
        low = s & -s
        got[s] = swap(got[s - low], "col", n_col, low)
    panel = [jnp.concatenate([got[s] for s in range(n_col // 2 * g, n_col // 2 * (g + 1))]) for g in range(2)]
    summed = []
    for g in range(2):
        product = dot(panel[g], trailing)
        check = dot(sums, panel[g], ((1,), (1,)))
        blocks = [
            jnp.concatenate(
                [
                    product[h * half : (h + 1) * half],
                    jnp.pad(check[:, h * half : (h + 1) * half], ((0, EXTRA - check.shape[0]), (0, columns - half))),
                ]
            )
            for h in range(2)
        ]
        keep = jnp.where(side == 0, blocks[0], blocks[1])
        send = jnp.where(side == 0, blocks[1], blocks[0])
        total = keep + swap(send, "row", n_row, 1)
        distance = 2
        while distance < n_row:
            total = total + swap(total, "row", n_row, distance)
            distance *= 2
        summed += [total, swap(total, "row", n_row, 1)]
    factor = xor_blocks(factor, 1, n_col, col)
    factor = xor_blocks(factor, 0, n_col, col ^ (side * (n_col // 4)))
    whole = jnp.concatenate(panel)
    spread = dot(whole, factor, ((0,), (1,)))
    coeff = dot(check_weights(rows), spread)
    main = jnp.concatenate([part[:half] for part in summed])
    check = jnp.concatenate([part[half : half + sums.shape[0], :half] for part in summed], axis=1)
    updated = trailing - dot(spread, main)
    column_checks = (sums - dot(check, spread, ((1,), (1,)))).T
    row_checks = row_sums - dot(coeff, main)
    return (updated, column_checks, row_checks)


def solution(mesh):
    n_row, n_col = mesh.shape["row"], mesh.shape["col"]
    fits = n_col >= 4 and n_col & (n_col - 1) == 0 and n_row >= 2 and n_row & (n_row - 1) == 0

    def shards(*args):
        return steps(n_row, n_col, *args) if fits else plain(*args)

    placed = (P("row", "col"), P("row", "col"), P(), P("row", "col"), P("row", "col"))
    return jax.shard_map(
        shards,
        mesh=mesh,
        in_specs=placed,
        out_specs=(P("row", "col"), P("row", "col"), P("row", "col")),
        check_vma=False,
    )
```

time: 139 us -> 43.9 us (0.32)
  waiting for transfers between devices: 83.6 us -> 13.4 us
  blocking collectives: 21.3 us -> 0 us
  starting transfers between devices: 0.08 us -> 18.8 us
  between operations: 14.1 us -> 0.95 us
  local copies, waits for them, and re-layouts: 7.89 us -> 2.82 us
  matrix products: 12.2 us -> 7.4 us
    psum x1 -> x0, waiting for transfers between devices: 65.9 us -> none  [shards(): summed_main, summed_check = lax.psum((product_main, product_check), 'row')]
    psum x1 -> x0, blocking collectives: 21.3 us -> none  [shards(): summed_main, summed_check = lax.psum((product_main, product_check), 'row')]
    ppermute x0 -> x11, starting transfers between devices: none -> 18.8 us  [swap(): return lax.ppermute(value, axis, [(i, i ^ distance) for i in range(size)])]
    all_gather x1 -> x0, waiting for transfers between devices: 17 us -> none  [shards(): panel = lax.all_gather(reflectors, 'col', axis=1, tiled=True)]
    ppermute x0 -> x11, waiting for transfers between devices: none -> 13.4 us  [swap(): return lax.ppermute(value, axis, [(i, i ^ distance) for i in range(size)])]
    unnamed x15 -> x10, local copies, waits for them, and re-layouts: 7.12 us -> 1.49 us
    dot_general x7 -> x9, matrix products: 12.2 us -> 7.4 us  [dot(): lax.dot_general(left, right, (dims, ((), ())), precision=lax.Precision.HI...]
  transfers between devices with their start and end apart: 2 -> 11, of which waited for: 2 -> 8; matrix products, arithmetic and copies ran while one was open for 5% -> 14% of each run, Pallas kernels for 0% -> 0%
where the time goes in v1:
time: 43.9 us; the launch traced here: 43.7 us
  starting transfers between devices  18.8 us (43%)
  waiting for transfers between devices  13.4 us (31%)
  matrix products  7.4 us (17%)
  local copies, waits for them, and re-layouts  2.82 us (6%)
  between operations  0.95 us (2%)
    ppermute x11, starting transfers between devices, swap(): return lax.ppermute(value, axis, [(i, i ^ distance) for i in range(size)])  18.8 us
    ppermute x11, waiting for transfers between devices, swap(): return lax.ppermute(value, axis, [(i, i ^ distance) for i in range(size)])  13.4 us
    dot_general x9, matrix products, dot(): lax.dot_general(left, right, (dims, ((), ())), precision=lax.Precision.HI...  7.4 us
    unnamed x10, local copies, waits for them, and re-layouts  1.49 us
  transfers between devices with their start and end apart: 11, of which 8 were waited for; matrix products, arithmetic and copies ran while one was open for 14% of the time, Pallas kernels for 0%

profile of v1, /device:TPU:0, one launch (start us, length us, event | category | flops | bytes accessed | tf_op | source)
XLA Modules:
  0.0 43.7 jit_solution(6927130321637046635)
XLA Ops:
  0.6 3.1 %collective-permute-start.1 = (f32[64,1024]{1,0:T(8,128)}, f32[64,1024]{1,0:T(8,128)S(1)}, u32[]{:S(2)}, u32[]{:S(2)}) collective-permute-start(f32[64,1024]{1,0:T(8,128)} %bitcast.33), channel_id=1, source_target_pairs={{0,2},{1,3},{2,0},{3,1},{4,6},{5,7},{6,4},{7,5},{8,10},{9,11},{10,... | collective-permute-start | bytes 786440 | tf_op jit(solution)/shard_map/ppermute | solution.py:14
  3.7 0.0 collective-permute-start
  3.7 1.1 %copy.10 = f32[256,256]{0,1:T(8,128)S(1)} copy(f32[256,256]{1,0:T(8,128)} %param.7) | data formatting | bytes 524288 | tf_op args[2]
  5.0 0.1 copy.12
  5.1 0.0 copy-start
  5.1 0.0 copy-start.1
  5.2 0.1 copy.13
  5.3 0.1 reshape.49
  5.5 0.0 copy-start.2
  5.5 0.6 %rev.19 = f32[1,2,128,256]{2,1,3,0:T(2,128)S(1)} reverse(f32[1,2,128,256]{2,1,3,0:T(2,128)S(1)} %reshape.49), dimensions={1} | reverse | bytes 524288 | tf_op jit(solution)/shard_map/jit(_flip)/rev | solution.py:23
  6.2 0.0 collective-permute-done
  6.2 0.4 copy-done
  6.5 0.0 copy-done.1
  6.5 0.7 %fusion.8 = f32[128,384]{1,0:T(8,128)S(1)} fusion(f32[1024,384]{1,0:T(8,128)S(1)} %copy-done, f32[64,1024]{1,0:T(8,128)S(1)} %collective-permute-done, f32[64,1024]{1,0:T(8,128)S(1)} %bitcast.35), kind=kOutput, calls=%fused_computation.14 | convolution fusion | flops 302120960 | bytes 2293760 | tf_op jit(solution)/shard_map/dot_general | solution.py:10
  7.2 3.0 %collective-permute-done.1 = f32[64,1024]{1,0:T(8,128)S(1)} collective-permute-done((f32[64,1024]{1,0:T(8,128)}, f32[64,1024]{1,0:T(8,128)S(1)}, u32[]{:S(2)}, u32[]{:S(2)}) %collective-permute-start.1) | collective-permute-done | bytes 262176 | tf_op jit(solution)/shard_map/ppermute | solution.py:14
  10.2 0.0 collective-permute-start.2
  10.2 0.0 copy-done.2
  10.2 0.3 convolution_bitcast_fusion.1
  10.5 0.1 fusion.31
  10.6 1.8 %collective-permute-start.3 = (f32[72,384]{1,0:T(8,128)S(1)}, f32[72,384]{1,0:T(8,128)S(1)}, u32[]{:S(2)}, u32[]{:S(2)}) collective-permute-start(f32[72,384]{1,0:T(8,128)S(1)} %fusion.11), channel_id=1, source_target_pairs={{0,4},{4,0},{8,12},{12,8},{16,20},{20,16},{24,28},{28,24},{1,5},{5... | collective-permute-start | bytes 331784 | tf_op jit(solution)/shard_map/ppermute | solution.py:14
  12.4 0.0 collective-permute-done.2
  12.5 0.3 convolution_bitcast_fusion
  12.8 0.7 %fusion.33 = f32[128,384]{1,0:T(8,128)S(1)} fusion(f32[128,1024]{1,0:T(8,128)S(1)} %constant_dynamic-update-slice_fusion, f32[1024,384]{1,0:T(8,128)S(1)} %copy-done), kind=kOutput, calls=%fused_computation.54 | convolution fusion | flops 301989888 | bytes 2293760 | tf_op jit(solution)/shard_map/dot_general | solution.py:10
  13.5 0.1 fusion.32
  13.6 1.1 %collective-permute-start.7 = (f32[72,384]{1,0:T(8,128)S(1)}, f32[72,384]{1,0:T(8,128)S(1)}, u32[]{:S(2)}, u32[]{:S(2)}) collective-permute-start(f32[72,384]{1,0:T(8,128)S(1)} %fusion.12), channel_id=1, source_target_pairs={{0,4},{4,0},{8,12},{12,8},{16,20},{20,16},{24,28},{28,24},{1,5},{5... | collective-permute-start | bytes 331784 | tf_op jit(solution)/shard_map/ppermute | solution.py:14
  14.6 1.5 %collective-permute-done.3 = f32[72,384]{1,0:T(8,128)S(1)} collective-permute-done((f32[72,384]{1,0:T(8,128)S(1)}, f32[72,384]{1,0:T(8,128)S(1)}, u32[]{:S(2)}, u32[]{:S(2)}) %collective-permute-start.3) | collective-permute-done | bytes 110624 | tf_op jit(solution)/shard_map/ppermute | solution.py:14
  16.2 1.9 %collective-permute-start.4 = (f32[72,384]{1,0:T(8,128)S(1)}, f32[72,384]{1,0:T(8,128)S(1)}, u32[]{:S(2)}, u32[]{:S(2)}) collective-permute-start(f32[72,384]{1,0:T(8,128)S(1)} %select_add_fusion.1), channel_id=1, source_target_pairs={{0,8},{4,12},{8,0},{12,4},{16,24},{20,28},{24,16},{28,20},{1,9},{5... | collective-permute-start | bytes 331784 | tf_op jit(solution)/shard_map/ppermute | solution.py:14
  18.1 0.8 %collective-permute-done.7 = f32[72,384]{1,0:T(8,128)S(1)} collective-permute-done((f32[72,384]{1,0:T(8,128)S(1)}, f32[72,384]{1,0:T(8,128)S(1)}, u32[]{:S(2)}, u32[]{:S(2)}) %collective-permute-start.7) | collective-permute-done | bytes 110624 | tf_op jit(solution)/shard_map/ppermute | solution.py:14
  18.8 1.6 %collective-permute-start.8 = (f32[72,384]{1,0:T(8,128)S(1)}, f32[72,384]{1,0:T(8,128)S(1)}, u32[]{:S(2)}, u32[]{:S(2)}) collective-permute-start(f32[72,384]{1,0:T(8,128)S(1)} %select_add_fusion), channel_id=1, source_target_pairs={{0,8},{4,12},{8,0},{12,4},{16,24},{20,28},{24,16},{28,20},{1,9},{5... | collective-permute-start | bytes 331784 | tf_op jit(solution)/shard_map/ppermute | solution.py:14
  20.5 0.6 %collective-permute-done.4 = f32[72,384]{1,0:T(8,128)S(1)} collective-permute-done((f32[72,384]{1,0:T(8,128)S(1)}, f32[72,384]{1,0:T(8,128)S(1)}, u32[]{:S(2)}, u32[]{:S(2)}) %collective-permute-start.4) | collective-permute-done | bytes 110624 | tf_op jit(solution)/shard_map/ppermute | solution.py:14
  21.1 3.1 %collective-permute-start.5 = (f32[72,384]{1,0:T(8,128)S(1)}, f32[72,384]{1,0:T(8,128)S(1)}, u32[]{:S(2)}, u32[]{:S(2)}) collective-permute-start(f32[72,384]{1,0:T(8,128)S(1)} %add.67), channel_id=1, source_target_pairs={{0,16},{4,20},{8,24},{12,28},{16,0},{20,4},{24,8},{28,12},{1,17},{... | collective-permute-start | bytes 331784 | tf_op jit(solution)/shard_map/ppermute | solution.py:14
  24.2 0.6 %collective-permute-done.8 = f32[72,384]{1,0:T(8,128)S(1)} collective-permute-done((f32[72,384]{1,0:T(8,128)S(1)}, f32[72,384]{1,0:T(8,128)S(1)}, u32[]{:S(2)}, u32[]{:S(2)}) %collective-permute-start.8) | collective-permute-done | bytes 110624 | tf_op jit(solution)/shard_map/ppermute | solution.py:14
  24.9 2.6 %collective-permute-start.9 = (f32[72,384]{1,0:T(8,128)S(1)}, f32[72,384]{1,0:T(8,128)S(1)}, u32[]{:S(2)}, u32[]{:S(2)}) collective-permute-start(f32[72,384]{1,0:T(8,128)S(1)} %add.70), channel_id=1, source_target_pairs={{0,16},{4,20},{8,24},{12,28},{16,0},{20,4},{24,8},{28,12},{1,17},{... | collective-permute-start | bytes 331784 | tf_op jit(solution)/shard_map/ppermute | solution.py:14
  27.5 1.0 %fusion = f32[1024,256]{1,0:T(8,128)S(1)} fusion(f32[64,1024]{1,0:T(8,128)S(1)} %collective-permute-done.2, f32[64,1024]{1,0:T(8,128)S(1)} %collective-permute-done.1, f32[64,1024]{1,0:T(8,128)S(1)} %collective-permute-done, f32[64,1024]{1,0:T(8,128)S(1)} %bitcast.37, f32[256,256]{0,1:T(8,128)S(1)} %broadcast_select_fusion, ...), kind=kOutput, calls=%fused_computation.5 | convolution fusion | flops 403505152 | bytes 2621441 | tf_op jit(solution)/shard_map/dot_general | solution.py:10
  28.5 3.7 %collective-permute-done.5 = f32[72,384]{1,0:T(8,128)S(1)} collective-permute-done((f32[72,384]{1,0:T(8,128)S(1)}, f32[72,384]{1,0:T(8,128)S(1)}, u32[]{:S(2)}, u32[]{:S(2)}) %collective-permute-start.5) | collective-permute-done | bytes 110624 | tf_op jit(solution)/shard_map/ppermute | solution.py:14
  32.2 2.6 %collective-permute-start.6 = (f32[72,384]{1,0:T(8,128)S(1)}, f32[72,384]{1,0:T(8,128)S(1)}, u32[]{:S(2)}, u32[]{:S(2)}) collective-permute-start(f32[72,384]{1,0:T(8,128)S(1)} %add.68), channel_id=1, source_target_pairs={{0,4},{4,0},{8,12},{12,8},{16,20},{20,16},{24,28},{28,24},{1,5},{5... | collective-permute-start | bytes 331784 | tf_op jit(solution)/shard_map/ppermute | solution.py:14
  34.7 0.0 collective-permute-done.9
  34.8 1.2 %collective-permute-start.10 = (f32[72,384]{1,0:T(8,128)S(1)}, f32[72,384]{1,0:T(8,128)S(1)}, u32[]{:S(2)}, u32[]{:S(2)}) collective-permute-start(f32[72,384]{1,0:T(8,128)S(1)} %add.71), channel_id=1, source_target_pairs={{0,4},{4,0},{8,12},{12,8},{16,20},{20,16},{24,28},{28,24},{1,5},{5... | collective-permute-start | bytes 331784 | tf_op jit(solution)/shard_map/ppermute | solution.py:14
  35.9 0.4 fusion.13
  36.4 1.8 %collective-permute-done.6 = f32[72,384]{1,0:T(8,128)S(1)} collective-permute-done((f32[72,384]{1,0:T(8,128)S(1)}, f32[72,384]{1,0:T(8,128)S(1)}, u32[]{:S(2)}, u32[]{:S(2)}) %collective-permute-start.6) | collective-permute-done | bytes 110624 | tf_op jit(solution)/shard_map/ppermute | solution.py:14
  38.2 1.4 %collective-permute-done.10 = f32[72,384]{1,0:T(8,128)S(1)} collective-permute-done((f32[72,384]{1,0:T(8,128)S(1)}, f32[72,384]{1,0:T(8,128)S(1)}, u32[]{:S(2)}, u32[]{:S(2)}) %collective-permute-start.10) | collective-permute-done | bytes 110624 | tf_op jit(solution)/shard_map/ppermute | solution.py:14
  39.6 0.0 copy-start.3
  39.6 2.1 %convolution_subtract_fusion = f32[1024,384]{1,0:T(8,128)} fusion(f32[1024,384]{1,0:T(8,128)S(1)} %copy-done, f32[1024,256]{1,0:T(8,128)S(1)} %fusion, f32[64,384]{1,0:T(8,128)S(1)} %slice.71, f32[64,384]{1,0:T(8,128)S(1)} %slice.70, f32[64,384]{1,0:T(8,128)S(1)} %slice.67, f32[64,384]{1,0:T(8,128)S(1)} %slice.66), kind=kOutput, calls=%fused_computation | convolution fusion | flops 604667904 | bytes 4587520 | tf_op jit(solution)/shard_map/dot_general | solution.py:10
  41.7 0.0 copy-done.3
  41.7 0.8 %convolution_subtract_fusion.2 = f32[2,384]{1,0:T(2,128)} fusion(f32[2,384]{1,0:T(2,128)S(1)} %copy-done.3, f32[2,256]{1,0:T(2,128)S(1)} %fusion.13, f32[64,384]{1,0:T(8,128)S(1)} %slice.71, f32[64,384]{1,0:T(8,128)S(1)} %slice.70, f32[64,384]{1,0:T(8,128)S(1)} %slice.67, f32[64,384]{1,0:T(8,128)S(1)} %slice.66), kind=kOutput, calls=%fused_computation.2 | convolution fusion | flops 1475328 | bytes 401408 | tf_op jit(solution)/shard_map/dot_general | solution.py:10
  42.5 1.1 %convolution_subtract_fusion.1 = f32[1024,2]{0,1:T(2,128)} fusion(f32[1024,2]{0,1:T(2,128)S(1)} %copy-done.2, f32[1024,256]{1,0:T(8,128)S(1)} %fusion, f32[2,64]{1,0:T(2,128)S(1)} %slice.75, f32[2,64]{1,0:T(2,128)S(1)} %slice.74, f32[2,64]{1,0:T(2,128)S(1)} %slice.73, f32[2,64]{1,0:T(2,128)S(1)} %slice.72), kind=kOutput, calls=%fused_computation.1 | convolution fusion | flops 3149312 | bytes 1067008 | tf_op jit(solution)/shard_map/dot_general | solution.py:10
  (27 shorter events, 0.4 us)
Async XLA Ops:
  0.6 9.6 %collective-permute-start.1 = (f32[64,1024]{1,0:T(8,128)}, f32[64,1024]{1,0:T(8,128)S(1)}, u32[]{:S(2)}, u32[]{:S(2)}) collective-permute-start(f32[64,1024]{1,0:T(8,128)} %bitcast.33), channel_id=1, source_target_pairs={{0,2},{1,3},{2,0},{3,1},{4,6},{5,7},{6,4},{7,5},{8,10},{9,11},{10,... | collective-permute-start | bytes 786440 | tf_op jit(solution)/shard_map/ppermute | solution.py:14
  3.7 2.5 %collective-permute-start = (f32[64,1024]{1,0:T(8,128)}, f32[64,1024]{1,0:T(8,128)S(1)}, u32[]{:S(2)}, u32[]{:S(2)}) collective-permute-start(f32[64,1024]{1,0:T(8,128)} %bitcast.34), channel_id=1, source_target_pairs={{0,1},{1,0},{2,3},{3,2},{4,5},{5,4},{6,7},{7,6},{8,9},{9,8},{10,11... | collective-permute-start | bytes 786440 | tf_op jit(solution)/shard_map/ppermute | solution.py:14
  5.1 1.4 %copy-start = (f32[1024,384]{1,0:T(8,128)S(1)}, f32[1024,384]{1,0:T(8,128)}, u32[]{:S(2)}) copy-start(f32[1024,384]{1,0:T(8,128)} %param.5) | copy-start | bytes 4718596
  5.1 1.4 %copy-start.1 = (f32[1024,64]{0,1:T(8,128)S(1)}, f32[1024,64]{0,1:T(8,128)}, u32[]{:S(2)}) copy-start(f32[1024,64]{0,1:T(8,128)} %param.6) | copy-start | bytes 786436
  5.5 4.7 %copy-start.2 = (f32[1024,2]{0,1:T(2,128)S(1)}, f32[1024,2]{0,1:T(2,128)}, u32[]{:S(2)}) copy-start(f32[1024,2]{0,1:T(2,128)} %param.8) | copy-start | bytes 24580
  10.2 2.2 %collective-permute-start.2 = (f32[64,1024]{1,0:T(8,128)S(1)}, f32[64,1024]{1,0:T(8,128)S(1)}, u32[]{:S(2)}, u32[]{:S(2)}) collective-permute-start(f32[64,1024]{1,0:T(8,128)S(1)} %collective-permute-done.1), channel_id=1, source_target_pairs={{0,1},{1,0},{2,3},{3,2},{4,5},{5,4},{6,7},{7,6},{8,9},{9,8},{10,11... | collective-permute-start | bytes 786440 | tf_op jit(solution)/shard_map/ppermute | solution.py:14
  10.6 5.5 %collective-permute-start.3 = (f32[72,384]{1,0:T(8,128)S(1)}, f32[72,384]{1,0:T(8,128)S(1)}, u32[]{:S(2)}, u32[]{:S(2)}) collective-permute-start(f32[72,384]{1,0:T(8,128)S(1)} %fusion.11), channel_id=1, source_target_pairs={{0,4},{4,0},{8,12},{12,8},{16,20},{20,16},{24,28},{28,24},{1,5},{5... | collective-permute-start | bytes 331784 | tf_op jit(solution)/shard_map/ppermute | solution.py:14
  13.6 5.3 %collective-permute-start.7 = (f32[72,384]{1,0:T(8,128)S(1)}, f32[72,384]{1,0:T(8,128)S(1)}, u32[]{:S(2)}, u32[]{:S(2)}) collective-permute-start(f32[72,384]{1,0:T(8,128)S(1)} %fusion.12), channel_id=1, source_target_pairs={{0,4},{4,0},{8,12},{12,8},{16,20},{20,16},{24,28},{28,24},{1,5},{5... | collective-permute-start | bytes 331784 | tf_op jit(solution)/shard_map/ppermute | solution.py:14
  16.2 4.9 %collective-permute-start.4 = (f32[72,384]{1,0:T(8,128)S(1)}, f32[72,384]{1,0:T(8,128)S(1)}, u32[]{:S(2)}, u32[]{:S(2)}) collective-permute-start(f32[72,384]{1,0:T(8,128)S(1)} %select_add_fusion.1), channel_id=1, source_target_pairs={{0,8},{4,12},{8,0},{12,4},{16,24},{20,28},{24,16},{28,20},{1,9},{5... | collective-permute-start | bytes 331784 | tf_op jit(solution)/shard_map/ppermute | solution.py:14
  18.8 6.0 %collective-permute-start.8 = (f32[72,384]{1,0:T(8,128)S(1)}, f32[72,384]{1,0:T(8,128)S(1)}, u32[]{:S(2)}, u32[]{:S(2)}) collective-permute-start(f32[72,384]{1,0:T(8,128)S(1)} %select_add_fusion), channel_id=1, source_target_pairs={{0,8},{4,12},{8,0},{12,4},{16,24},{20,28},{24,16},{28,20},{1,9},{5... | collective-permute-start | bytes 331784 | tf_op jit(solution)/shard_map/ppermute | solution.py:14
  21.1 11.0 %collective-permute-start.5 = (f32[72,384]{1,0:T(8,128)S(1)}, f32[72,384]{1,0:T(8,128)S(1)}, u32[]{:S(2)}, u32[]{:S(2)}) collective-permute-start(f32[72,384]{1,0:T(8,128)S(1)} %add.67), channel_id=1, source_target_pairs={{0,16},{4,20},{8,24},{12,28},{16,0},{20,4},{24,8},{28,12},{1,17},{... | collective-permute-start | bytes 331784 | tf_op jit(solution)/shard_map/ppermute | solution.py:14
  24.9 9.9 %collective-permute-start.9 = (f32[72,384]{1,0:T(8,128)S(1)}, f32[72,384]{1,0:T(8,128)S(1)}, u32[]{:S(2)}, u32[]{:S(2)}) collective-permute-start(f32[72,384]{1,0:T(8,128)S(1)} %add.70), channel_id=1, source_target_pairs={{0,16},{4,20},{8,24},{12,28},{16,0},{20,4},{24,8},{28,12},{1,17},{... | collective-permute-start | bytes 331784 | tf_op jit(solution)/shard_map/ppermute | solution.py:14
  32.2 5.9 %collective-permute-start.6 = (f32[72,384]{1,0:T(8,128)S(1)}, f32[72,384]{1,0:T(8,128)S(1)}, u32[]{:S(2)}, u32[]{:S(2)}) collective-permute-start(f32[72,384]{1,0:T(8,128)S(1)} %add.68), channel_id=1, source_target_pairs={{0,4},{4,0},{8,12},{12,8},{16,20},{20,16},{24,28},{28,24},{1,5},{5... | collective-permute-start | bytes 331784 | tf_op jit(solution)/shard_map/ppermute | solution.py:14
  34.8 4.8 %collective-permute-start.10 = (f32[72,384]{1,0:T(8,128)S(1)}, f32[72,384]{1,0:T(8,128)S(1)}, u32[]{:S(2)}, u32[]{:S(2)}) collective-permute-start(f32[72,384]{1,0:T(8,128)S(1)} %add.71), channel_id=1, source_target_pairs={{0,4},{4,0},{8,12},{12,8},{16,20},{20,16},{24,28},{28,24},{1,5},{5... | collective-permute-start | bytes 331784 | tf_op jit(solution)/shard_map/ppermute | solution.py:14
  39.6 2.2 %copy-start.3 = (f32[2,384]{1,0:T(2,128)S(1)}, f32[2,384]{1,0:T(2,128)}, u32[]{:S(2)}) copy-start(f32[2,384]{1,0:T(2,128)} %param.9) | copy-start | bytes 9220

commit v2 on v0

v2 whole, which is shorter than its diff:
```python
import jax
import jax.numpy as jnp
from jax import lax
from jax.experimental import pallas as pl
from jax.experimental.pallas import tpu as pltpu
from jax.sharding import PartitionSpec as P

EXTRA = 8
ORDERS = lambda b: (b, b[1:] + b[:1])
BLOCKS = (4, 2)
LOADS = 4
VMEM = 16777216
LIMIT = pltpu.CompilerParams(vmem_limit_bytes=VMEM)
ROWS = ((1,), (0,))
LANES = ((1,), (1,))


def dot(left, right, dims=ROWS):
    return lax.dot_general(left, right, (dims, ((), ())), precision=lax.Precision.HIGH, preferred_element_type=jnp.float32)


def once(left, right, dims=ROWS):
    return lax.dot_general(left, right, (dims, ((), ())), preferred_element_type=jnp.float32)


def high_low(value):
    high = value.astype(jnp.bfloat16)
    return high, (value - high.astype(jnp.float32)).astype(jnp.bfloat16)


def thrice(left, right, dims=ROWS):
    return once(left[0], right[0], dims) + (once(left[0], right[1], dims) + once(left[1], right[0], dims))


def swap(value, axis, size, distance):
    return lax.ppermute(value, axis, [(i, i ^ distance) for i in range(size)])


def swap_mixed(value, n_row, n_col, distances):
    pairs = [(r * n_col + c, (r ^ distances[c % 2]) * n_col + c) for r in range(n_row) for c in range(n_col)]
    return lax.ppermute(value, ("row", "col"), pairs)


def check_weights(count):
    local = jnp.arange(count).astype(jnp.float32)
    scale = 1.0 / jnp.sqrt(jnp.float32(count))
    return jnp.stack([jnp.ones((count,), jnp.float32) * scale, (local + 1.0) * scale / count])


def plain(trailing, reflectors, factor, column_sums, row_sums):
    panel = lax.all_gather(reflectors, "col", axis=1, tiled=True)
    columns = trailing.shape[1]
    joined = jnp.concatenate([trailing, column_sums], axis=1)
    image = dot(factor.T, lax.psum(dot(panel.T, joined), "row"))
    joined = joined - dot(panel, image)
    coeff = dot(check_weights(trailing.shape[0]), panel)
    return (joined[:, :columns], joined[:, columns:], row_sums - dot(coeff, image[:, :columns]))


def put(ref, product, check):
    half = product.shape[0]
    ref[:half, :] = product
    ref[half:, :] = jnp.zeros((EXTRA, ref.shape[1]), jnp.float32)
    ref[half:, :half] = check


def tall_sums(sums_ref):
    count, rows = sums_ref.shape
    return jnp.concatenate([sums_ref[...], jnp.zeros((EXTRA - count, rows), jnp.float32)], axis=0)


def next_kernel(high_ref, low_ref, sums_ref, *refs):
    panel = high_low(jnp.concatenate([ref[...] for ref in refs[:-1]], axis=0))
    product = thrice(panel, (high_ref[...], low_ref[...]))
    put(refs[-1], product, thrice(high_low(tall_sums(sums_ref)), panel, LANES))


def first_kernel(trailing_ref, piece_ref, sums_ref, out_ref, high_ref, low_ref, load_ref, panel_ref, check_ref, sems):
    rows = trailing_ref.shape[0]
    chunk = rows // LOADS
    loads = [pltpu.make_async_copy(piece_ref, panel_ref, sems.at[LOADS]), pltpu.make_async_copy(sums_ref, check_ref, sems.at[LOADS + 1])]
    for i in range(LOADS):
        band = pl.ds(i * chunk, chunk)
        loads.append(pltpu.make_async_copy(trailing_ref.at[band], load_ref.at[band], sems.at[i]))
    for load in loads:
        load.start()
    loads[0].wait()
    loads[1].wait()
    panel = high_low(panel_ref[...])
    check = thrice(high_low(tall_sums(check_ref)), panel, LANES)
    product = jnp.zeros((panel[0].shape[0], trailing_ref.shape[1]), jnp.float32)
    for i in range(LOADS):
        loads[2 + i].wait()
        band = slice(i * chunk, (i + 1) * chunk)
        part = high_low(load_ref[band, :])
        high_ref[band, :], low_ref[band, :] = part
        product += thrice((panel[0][:, band], panel[1][:, band]), part)
    put(out_ref, product, check)


VMEM_SPEC = pl.BlockSpec(memory_space=pltpu.VMEM)


def first_products(trailing, piece, sums):
    out = jax.ShapeDtypeStruct((piece.shape[0] + EXTRA, trailing.shape[1]), jnp.float32)
    part = jax.ShapeDtypeStruct(trailing.shape, jnp.bfloat16)
    return pl.pallas_call(
        first_kernel,
        in_specs=[pl.BlockSpec(memory_space=pltpu.HBM)] * 3,
        out_specs=[VMEM_SPEC] * 3,
        out_shape=[out, part, part],
        scratch_shapes=[pltpu.VMEM(a.shape, a.dtype) for a in (trailing, piece, sums)] + [pltpu.SemaphoreType.DMA((LOADS + 2,))],
        compiler_params=LIMIT,
    )(*[pltpu.with_memory_space_constraint(a, pltpu.HBM) for a in (trailing, piece, sums)])


def next_products(trailing, sums, pieces):
    half = sum(piece.shape[0] for piece in pieces)
    return pl.pallas_call(
        next_kernel,
        in_specs=[VMEM_SPEC] * (3 + len(pieces)),
        out_specs=VMEM_SPEC,
        out_shape=jax.ShapeDtypeStruct((half + EXTRA, trailing[0].shape[1]), jnp.float32),
        compiler_params=LIMIT,
    )(*trailing, sums, *pieces)


def spread_kernel(places_ref, order_ref, factor_ref, *refs):
    pieces, (high_ref, low_ref, late_ref, coeff_ref), (panel_ref, turned_ref) = refs[:-6], refs[-6:-2], refs[-2:]
    width = pieces[0].shape[0]
    for s, piece in enumerate(pieces):
        panel_ref[pl.ds(pl.multiple_of(places_ref[s], width), width), :] = piece[...]
        turned_ref[s * width : (s + 1) * width, :] = factor_ref[pl.ds(pl.multiple_of(order_ref[s], width), width), :]
    panel = jnp.transpose(panel_ref[...])
    spread = thrice(high_low(panel), high_low(turned_ref[...]), LANES)
    high, low = high_low(spread)
    high_ref[...] = high
    low_ref[...] = low
    size = panel.shape[1]
    late = size - late_ref.shape[1] // 4
    late_ref[...] = jnp.concatenate([high[:, late:], high[:, late:], low[:, late:], low[:, late:]], axis=1)
    count = panel.shape[0]
    scale = 1.0 / jnp.sqrt(jnp.float32(count))
    local = lax.broadcasted_iota(jnp.int32, (EXTRA, count), 1).astype(jnp.float32)
    kind = lax.broadcasted_iota(jnp.int32, (EXTRA, count), 0)
    weights = jnp.where(kind == 0, scale, jnp.where(kind == 1, (local + 1.0) * scale / count, 0.0))
    coeff_ref[...] = thrice(high_low(weights), (high, low))


def spreads(places, order, factor, pieces, late):
    size, rows = factor.shape[0], pieces[0].shape[1]
    return pl.pallas_call(
        spread_kernel,
        in_specs=[pl.BlockSpec(memory_space=pltpu.SMEM)] * 2 + [pl.BlockSpec(memory_space=pltpu.VMEM)] * (1 + len(pieces)),
        out_specs=[pl.BlockSpec(memory_space=pltpu.VMEM)] * 4,
        out_shape=[
            jax.ShapeDtypeStruct((rows, size), jnp.bfloat16),
            jax.ShapeDtypeStruct((rows, size), jnp.bfloat16),
            jax.ShapeDtypeStruct((rows, 4 * late), jnp.bfloat16),
            jax.ShapeDtypeStruct((EXTRA, size), jnp.float32),
        ],
        scratch_shapes=[pltpu.VMEM((size, rows), jnp.float32), pltpu.VMEM((size, size), jnp.float32)],
        compiler_params=LIMIT,
    )(places, order, factor, *pieces)


def apply_kernel(acc_ref, high_ref, low_ref, coeff_ref, rows_ref, sums_ref, *refs):
    parts, (out_ref, row_ref, col_ref) = refs[:-3], refs[-3:]
    tall = parts[0].shape[0] - EXTRA
    upto = tall * len(parts)
    right = high_low(jnp.concatenate([part[:tall, :] for part in parts], axis=0))
    left = (high_ref[:, :upto], low_ref[:, :upto])
    out_ref[...] = acc_ref[...] - thrice(left, right)
    check = jnp.concatenate([part[tall:, :tall] for part in parts], axis=1)
    col_ref[...] = sums_ref[...] - thrice(high_low(check), left, LANES)[: col_ref.shape[0]]

    @pl.when(pl.program_id(0) == 0)
    def _():
        row_ref[...] = rows_ref[...] - thrice(high_low(coeff_ref[:, :upto]), right)[: row_ref.shape[0]]


def finish_kernel(acc_ref, left_ref, coeff_ref, rows_ref, sums_ref, part_ref, out_ref, row_ref, col_ref):
    tall = part_ref.shape[0] - EXTRA
    high, low = high_low(part_ref[:tall, :])
    right = jnp.concatenate([high, low, high, low], axis=0)
    left = left_ref[...]
    out_ref[...] = acc_ref[...] - once(left, right)
    high, low = high_low(part_ref[tall:, :tall])
    col_ref[...] = sums_ref[...] - once(jnp.concatenate([high, low, high, low], axis=1), left, LANES)[: col_ref.shape[0]]

    @pl.when(pl.program_id(0) == 0)
    def _():
        size = coeff_ref.shape[1]
        high, low = high_low(coeff_ref[:, size - tall :])
        row_ref[...] = rows_ref[...] - once(jnp.concatenate([high, high, low, low], axis=1), right)[: row_ref.shape[0]]


def update(kernel, blocks, acc, lefts, coeff, row_sums, sums, parts):
    rows, _ = acc.shape
    tall = rows // blocks
    band = lambda array: pl.BlockSpec((tall, array.shape[1]), lambda i: (i, 0))
    whole = lambda array: pl.BlockSpec(array.shape, lambda i: (0,) * array.ndim)
    lanes = pl.BlockSpec((sums.shape[0], tall), lambda i: (0, i))
    return pl.pallas_call(
        kernel,
        grid=(blocks,),
        in_specs=[band(acc)] + [band(left) for left in lefts] + [whole(coeff), whole(row_sums), lanes] + [whole(part) for part in parts],
        out_specs=[band(acc), whole(row_sums), lanes],
        out_shape=[jax.ShapeDtypeStruct(a.shape, a.dtype) for a in (acc, row_sums, sums)],
        compiler_params=LIMIT,
    )(acc, *lefts, coeff, row_sums, sums, *parts)


def near(start, count, n_col):
    got = [start]
    for k in range(1, count):
        low = k & -k
        got.append(swap(got[k - low], "col", n_col, low))
    return got


def steps(n_row, n_col, trailing, reflectors, factor, column_sums, row_sums):
    width = reflectors.shape[1]
    row = lax.axis_index("row")
    col = lax.axis_index("col")
    half, quarter = n_col // 2, n_col // 4
    sums = column_sums.T
    bits = [1 << b for b in range(n_row.bit_length() - 1)]
    other = swap(reflectors.T, "col", n_col, half)
    mine = near(reflectors.T, half, n_col)
    own, high, low = first_products(trailing, mine[0], sums)
    others = near(other, half, n_col)
    summed = []
    order = []
    for g, pieces in enumerate((mine, others)):
        ways = list(zip(*ORDERS(bits)))
        side = jnp.where(col % 2 == 0, row // ways[0][0], row // ways[0][1]) % 2
        if g == 0 and quarter == 1:
            parts = [own]
        else:
            parts = [next_products((high, low), sums, pieces[:quarter])]
        parts.append(next_products((high, low), sums, pieces[quarter:]))
        total = jnp.where(side == 0, parts[0], parts[1])
        value = jnp.where(side == 0, parts[1], parts[0])
        for way in ways:
            total = total + swap_mixed(value, n_row, n_col, way)
            value = total
        summed += [total, swap_mixed(total, n_row, n_col, ways[0])]
        order.append((jnp.arange(half) + g * half) ^ col ^ (side * quarter))
    places = (jnp.arange(n_col) ^ col) * width
    order = jnp.concatenate(order) * width
    late = quarter * width
    high, low, last, coeff = spreads(places, order, factor, mine + others, late)
    acc, row_sums, sums = update(apply_kernel, BLOCKS[0], trailing, (high, low), coeff, row_sums, sums, summed[:-1])
    updated, row_checks, sums = update(finish_kernel, BLOCKS[1], acc, (last,), coeff, row_sums, sums, summed[-1:])
    return (updated, sums.T, row_checks)


def solution(mesh):
    n_row, n_col = mesh.shape["row"], mesh.shape["col"]
    fits = n_col >= 4 and n_col & (n_col - 1) == 0 and n_row >= 2 and n_row & (n_row - 1) == 0

    def shards(*args):
        return steps(n_row, n_col, *args) if fits else plain(*args)

    placed = (P("row", "col"), P("row", "col"), P(), P("row", "col"), P("row", "col"))
    return jax.shard_map(
        shards,
        mesh=mesh,
        in_specs=placed,
        out_specs=(P("row", "col"), P("row", "col"), P("row", "col")),
        check_vma=False,
    )
```

time: 139 us -> 39.6 us (0.28)
  waiting for transfers between devices: 83.6 us -> 12.3 us
  blocking collectives: 21.3 us -> 0 us
  starting transfers between devices: 0.08 us -> 16.5 us
  between operations: 14.1 us -> 0.79 us
  matrix products: 12.2 us -> 0 us
  Pallas kernels: 0 us -> 9.62 us
  local copies, waits for them, and re-layouts: 7.89 us -> 0.04 us
    psum x1 -> x0, waiting for transfers between devices: 65.9 us -> none  [shards(): summed_main, summed_check = lax.psum((product_main, product_check), 'row')]
    psum x1 -> x0, blocking collectives: 21.3 us -> none  [shards(): summed_main, summed_check = lax.psum((product_main, product_check), 'row')]
    all_gather x1 -> x0, waiting for transfers between devices: 17 us -> none  [shards(): panel = lax.all_gather(reflectors, 'col', axis=1, tiled=True)]
    ppermute x0 -> x11, starting transfers between devices: none -> 16.5 us  [the longest x8 13.4 us: swap_mixed(): return lax.ppermute(value, ('row', 'col'), pairs)]
    ppermute x0 -> x11, waiting for transfers between devices: none -> 12.3 us  [the longest x3 6.52 us: swap(): return lax.ppermute(value, axis, [(i, i ^ distance) for i in range(size)])]
    dot_general x7 -> x0, matrix products: 12.2 us -> none  [matmul(): jnp.dot(left, right, precision=lax.Precision.HIGHEST, preferred_element_t...]
    pallas_call x0 -> x7, Pallas kernels: none -> 9.62 us  [the longest x2 3.66 us: update(): pl.pallas_call(kernel, grid=(blocks,), in_specs=[band(acc)] + [band(left)...]
    unnamed x15 -> x10, local copies, waits for them, and re-layouts: 7.12 us -> 0.04 us
  transfers between devices with their start and end apart: 2 -> 11, of which waited for: 2 -> 7; matrix products, arithmetic and copies ran while one was open for 5% -> 1% of each run, Pallas kernels for 0% -> 20%
where the time goes in v2:
time: 39.6 us; the launch traced here: 39.4 us
  starting transfers between devices  16.5 us (42%)
  waiting for transfers between devices  12.3 us (31%)
  Pallas kernels  9.62 us (24%)
  between operations  0.79 us (2%)
    ppermute x8, starting transfers between devices, swap_mixed(): return lax.ppermute(value, ('row', 'col'), pairs)  13.4 us
    ppermute x3, waiting for transfers between devices, swap(): return lax.ppermute(value, axis, [(i, i ^ distance) for i in range(size)])  6.52 us
    ppermute x8, waiting for transfers between devices, swap_mixed(): return lax.ppermute(value, ('row', 'col'), pairs)  5.77 us
    pallas_call x2, Pallas kernels, update(): pl.pallas_call(kernel, grid=(blocks,), in_specs=[band(acc)] + [band(left)...  3.66 us
    ppermute x3, starting transfers between devices, swap(): return lax.ppermute(value, axis, [(i, i ^ distance) for i in range(size)])  3.07 us
    pallas_call x1, Pallas kernels, first_products(): pl.pallas_call(first_kernel, in_specs=[pl.BlockSpec(memory_space=pltpu.HB...  2.26 us
    pallas_call x1, Pallas kernels, spreads(): pl.pallas_call(spread_kernel, in_specs=[pl.BlockSpec(memory_space=pltpu.S...  1.9 us
    pallas_call x3, Pallas kernels, next_products(): pl.pallas_call(next_kernel, in_specs=[VMEM_SPEC] * (3 + len(pieces)), out...  1.8 us
  transfers between devices with their start and end apart: 11, of which 7 were waited for; matrix products, arithmetic and copies ran while one was open for 1% of the time, Pallas kernels for 20%

profile of v2, /device:TPU:0, one launch (start us, length us, event | category | flops | bytes accessed | tf_op | source)
XLA Modules:
  0.0 39.4 jit_solution(11656081246835523595)
XLA Ops:
  0.6 0.0 copy-start.3
  0.6 3.1 %collective-permute-start.1 = (f32[64,1024]{1,0:T(8,128)}, f32[64,1024]{1,0:T(8,128)S(1)}, u32[]{:S(2)}, u32[]{:S(2)}) collective-permute-start(f32[64,1024]{1,0:T(8,128)} %bitcast.3), channel_id=1, source_target_pairs={{0,2},{1,3},{2,0},{3,1},{4,6},{5,7},{6,4},{7,5},{8,10},{9,11},{10,... | collective-permute-start | bytes 786440 | tf_op jit(solution)/shard_map/ppermute | solution.py:36
  3.7 0.0 collective-permute-start
  3.7 6.5 %collective-permute-done.1.refs_2_.refs_0_ = f32[64,1024]{1,0:T(8,128)S(1)} collective-permute-done((f32[64,1024]{1,0:T(8,128)}, f32[64,1024]{1,0:T(8,128)S(1)}, u32[]{:S(2)}, u32[]{:S(2)}) %collective-permute-start.1) | collective-permute-done | bytes 262176 | tf_op jit(solution)/shard_map/ppermute | solution.py:36
  10.2 0.0 collective-permute-start.2
  10.2 2.3 %shard_map.77 = (f32[72,384]{1,0:T(8,128)S(1)}, bf16[1024,384]{1,0:T(8,128)(2,1)S(1)}, bf16[1024,384]{1,0:T(8,128)(2,1)S(1)}) custom-call(f32[1024,384]{1,0:T(8,128)} %acc_ref.1, f32[64,1024]{1,0:T(8,128)} %bitcast.5, f32[2,1024]{1,0:T(2,128)} %bitcast.7), custom_call_target="tpu_custom_call" | custom-call | tf_op jit(solution)/shard_map/pallas_call | solution.py:107
  12.5 0.0 collective-permute-done.refs_1_.refs_0_
  12.5 0.0 copy-done.3
  12.5 0.6 %shard_map.78 = f32[72,384]{1,0:T(8,128)S(1)} custom-call(bf16[1024,384]{1,0:T(8,128)(2,1)S(1)} %get-tuple-element.20.high_ref, bf16[1024,384]{1,0:T(8,128)(2,1)S(1)} %get-tuple-element.21.low_ref, f32[2,1024]{1,0:T(2,128)S(1)} %bitcast.8, f32[64,1024]{1,0:T(8,128)S(1)} %collective-permute-done.refs_1_.refs_0_), custom_call_target="tpu_custom_call" | custom-call | tf_op jit(solution)/shard_map/pallas_call | solution.py:119
  13.1 1.8 %collective-permute-start.3 = (f32[72,384]{1,0:T(8,128)S(1)}, f32[72,384]{1,0:T(8,128)S(1)}, u32[]{:S(2)}, u32[]{:S(2)}) collective-permute-start(f32[72,384]{1,0:T(8,128)S(1)} %broadcast_select_fusion.1), channel_id=1, source_target_pairs={{0,4},{1,9},{2,6},{3,11},{4,0},{5,13},{6,2},{7,15},{8,12},{9,1},{1... | collective-permute-start | bytes 331784 | tf_op jit(solution)/shard_map/ppermute | solution.py:41
  14.9 0.6 %shard_map.79 = f32[72,384]{1,0:T(8,128)S(1)} custom-call(bf16[1024,384]{1,0:T(8,128)(2,1)S(1)} %get-tuple-element.20.high_ref, bf16[1024,384]{1,0:T(8,128)(2,1)S(1)} %get-tuple-element.21.low_ref, f32[2,1024]{1,0:T(2,128)S(1)} %bitcast.9, f32[64,1024]{1,0:T(8,128)S(1)} %collective-permute-done.1.refs_2_.refs_0_), custom_call_target="tpu_custom_call" | custom-call | tf_op jit(solution)/shard_map/pallas_call | solution.py:119
  15.5 0.0 collective-permute-done.2.refs_3_.refs_0_
  15.5 0.6 %shard_map.80 = f32[72,384]{1,0:T(8,128)S(1)} custom-call(bf16[1024,384]{1,0:T(8,128)(2,1)S(1)} %get-tuple-element.20.high_ref, bf16[1024,384]{1,0:T(8,128)(2,1)S(1)} %get-tuple-element.21.low_ref, f32[2,1024]{1,0:T(2,128)S(1)} %bitcast.10, f32[64,1024]{1,0:T(8,128)S(1)} %collective-permute-done.2.refs_3_.refs_0_), custom_call_target="tpu_custom_call" | custom-call | tf_op jit(solution)/shard_map/pallas_call | solution.py:119
  16.1 0.0 copy-start.1
  16.2 0.0 copy-start.2
  16.2 0.4 collective-permute-start.7
  16.6 1.4 %collective-permute-done.3 = f32[72,384]{1,0:T(8,128)S(1)} collective-permute-done((f32[72,384]{1,0:T(8,128)S(1)}, f32[72,384]{1,0:T(8,128)S(1)}, u32[]{:S(2)}, u32[]{:S(2)}) %collective-permute-start.3) | collective-permute-done | bytes 110624 | tf_op jit(solution)/shard_map/ppermute | solution.py:41
  18.0 0.0 copy-start
  18.0 0.0 copy-start.4
  18.0 1.9 %collective-permute-start.4 = (f32[72,384]{1,0:T(8,128)S(1)}, f32[72,384]{1,0:T(8,128)S(1)}, u32[]{:S(2)}, u32[]{:S(2)}) collective-permute-start(f32[72,384]{1,0:T(8,128)S(1)} %select_add_fusion.1), channel_id=1, source_target_pairs={{0,8},{1,17},{2,10},{3,19},{4,12},{5,21},{6,14},{7,23},{8,0},{9,25... | collective-permute-start | bytes 331784 | tf_op jit(solution)/shard_map/ppermute | solution.py:41
  19.9 1.1 %collective-permute-done.7 = f32[72,384]{1,0:T(8,128)S(1)} collective-permute-done((f32[72,384]{1,0:T(8,128)S(1)}, f32[72,384]{1,0:T(8,128)S(1)}, u32[]{:S(2)}, u32[]{:S(2)}) %collective-permute-start.7) | collective-permute-done | bytes 110624 | tf_op jit(solution)/shard_map/ppermute | solution.py:41
  21.0 1.6 %collective-permute-start.8 = (f32[72,384]{1,0:T(8,128)S(1)}, f32[72,384]{1,0:T(8,128)S(1)}, u32[]{:S(2)}, u32[]{:S(2)}) collective-permute-start(f32[72,384]{1,0:T(8,128)S(1)} %select_add_fusion), channel_id=1, source_target_pairs={{0,8},{1,17},{2,10},{3,19},{4,12},{5,21},{6,14},{7,23},{8,0},{9,25... | collective-permute-start | bytes 331784 | tf_op jit(solution)/shard_map/ppermute | solution.py:41
  22.7 1.1 %collective-permute-done.4 = f32[72,384]{1,0:T(8,128)S(1)} collective-permute-done((f32[72,384]{1,0:T(8,128)S(1)}, f32[72,384]{1,0:T(8,128)S(1)}, u32[]{:S(2)}, u32[]{:S(2)}) %collective-permute-start.4) | collective-permute-done | bytes 110624 | tf_op jit(solution)/shard_map/ppermute | solution.py:41
  23.8 2.5 %collective-permute-start.5 = (f32[72,384]{1,0:T(8,128)S(1)}, f32[72,384]{1,0:T(8,128)S(1)}, u32[]{:S(2)}, u32[]{:S(2)}) collective-permute-start(f32[72,384]{1,0:T(8,128)S(1)} %add.36), channel_id=1, source_target_pairs={{0,16},{1,5},{2,18},{3,7},{4,20},{5,1},{6,22},{7,3},{8,24},{9,13},... | collective-permute-start | bytes 331784 | tf_op jit(solution)/shard_map/ppermute | solution.py:41
  26.2 0.1 collective-permute-done.8
  26.4 2.2 %collective-permute-start.9 = (f32[72,384]{1,0:T(8,128)S(1)}, f32[72,384]{1,0:T(8,128)S(1)}, u32[]{:S(2)}, u32[]{:S(2)}) collective-permute-start(f32[72,384]{1,0:T(8,128)S(1)} %add.39), channel_id=1, source_target_pairs={{0,16},{1,5},{2,18},{3,7},{4,20},{5,1},{6,22},{7,3},{8,24},{9,13},... | collective-permute-start | bytes 331784 | tf_op jit(solution)/shard_map/ppermute | solution.py:41
  28.5 0.9 %collective-permute-done.5 = f32[72,384]{1,0:T(8,128)S(1)} collective-permute-done((f32[72,384]{1,0:T(8,128)S(1)}, f32[72,384]{1,0:T(8,128)S(1)}, u32[]{:S(2)}, u32[]{:S(2)}) %collective-permute-start.5) | collective-permute-done | bytes 110624 | tf_op jit(solution)/shard_map/ppermute | solution.py:41
  29.5 1.6 %collective-permute-start.6 = (f32[72,384]{1,0:T(8,128)S(1)}, f32[72,384]{1,0:T(8,128)S(1)}, u32[]{:S(2)}, u32[]{:S(2)}) collective-permute-start(f32[72,384]{1,0:T(8,128)S(1)} %add.37.refs_0_), channel_id=1, source_target_pairs={{0,4},{1,9},{2,6},{3,11},{4,0},{5,13},{6,2},{7,15},{8,12},{9,1},{1... | collective-permute-start | bytes 331784 | tf_op jit(solution)/shard_map/ppermute | solution.py:41
  31.0 1.1 %collective-permute-done.9 = f32[72,384]{1,0:T(8,128)S(1)} collective-permute-done((f32[72,384]{1,0:T(8,128)S(1)}, f32[72,384]{1,0:T(8,128)S(1)}, u32[]{:S(2)}, u32[]{:S(2)}) %collective-permute-start.9) | collective-permute-done | bytes 110624 | tf_op jit(solution)/shard_map/ppermute | solution.py:41
  32.2 1.5 %collective-permute-start.10 = (f32[72,384]{1,0:T(8,128)S(1)}, f32[72,384]{1,0:T(8,128)S(1)}, u32[]{:S(2)}, u32[]{:S(2)}) collective-permute-start(f32[72,384]{1,0:T(8,128)S(1)} %add.40.refs_2_), channel_id=1, source_target_pairs={{0,4},{1,9},{2,6},{3,11},{4,0},{5,13},{6,2},{7,15},{8,12},{9,1},{1... | collective-permute-start | bytes 331784 | tf_op jit(solution)/shard_map/ppermute | solution.py:41
  33.7 0.1 add_multiply_fusion.order_ref
  33.8 0.0 copy-done.1
  33.8 0.0 copy-done.2
  33.8 1.9 %shard_map.76 = (bf16[1024,256]{1,0:T(8,128)(2,1)S(1)}, bf16[1024,256]{1,0:T(8,128)(2,1)S(1)}, bf16[1024,256]{1,0:T(8,128)(2,1)S(1)}, f32[8,256]{1,0:T(8,128)S(1)}) custom-call(s32[4]{0:T(128)S(1)} %xor_multiply_fusion.places_ref, s32[4]{0:T(128)S(1)} %add_multiply_fusion.order_ref, f32[256,256]{1,0:T(8,128)S(1)} %copy-done.2, f32[64,1024]{1,0:T(8,128)S(1)} %bitcast.6, ...), custom_call_target="tpu_custom_call" | custom-call | tf_op jit(solution)/shard_map/pallas_call | solution.py:152
  35.7 0.0 collective-permute-done.6.refs_1_
  35.7 0.0 copy-done
  35.7 0.0 copy-done.4
  35.7 2.0 %shard_map.81 = (f32[1024,384]{1,0:T(8,128)S(1)}, f32[2,384]{1,0:T(2,128)S(1)}, f32[2,1024]{1,0:T(2,128)S(1)}) custom-call(f32[1024,384]{1,0:T(8,128)S(1)} %copy-done, bf16[1024,256]{1,0:T(8,128)(2,1)S(1)} %get-tuple-element.16.high_ref, bf16[1024,256]{1,0:T(8,128)(2,1)S(1)} %get-tuple-element.17.low_ref, f32[8,256]{1,0:T(8,128)S(1)} %get-tuple-element.18.coeff_ref, ...), custom_call_target="tpu_custom_call" | custom-call | tf_op jit(solution)/shard_map/pallas_call | solution.py:204
  37.7 0.0 collective-permute-done.10.part_ref
  37.7 1.7 %shard_map.82 = (f32[1024,384]{1,0:T(8,128)}, f32[2,384]{1,0:T(2,128)}, f32[2,1024]{1,0:T(2,128)}) custom-call(f32[1024,384]{1,0:T(8,128)S(1)} %get-tuple-element.22.acc_ref, bf16[1024,256]{1,0:T(8,128)(2,1)S(1)} %get-tuple-element.23.left_ref, f32[8,256]{1,0:T(8,128)S(1)} %get-tuple-element.18.coeff_ref, f32[2,384]{1,0:T(2,128)S(1)} %get-tuple-element.24.rows_ref, ...), custom_call_target="tpu_custom_call" | custom-call | tf_op jit(solution)/shard_map/pallas_call | solution.py:204
  (10 shorter events, 0.1 us)
Async XLA Ops:
  0.6 11.9 %copy-start.3 = (f32[1024,2]{0,1:T(2,128)S(1)}, f32[1024,2]{0,1:T(2,128)}, u32[]{:S(2)}) copy-start(f32[1024,2]{0,1:T(2,128)} %param.8) | copy-start | bytes 24580
  0.6 9.6 %collective-permute-start.1 = (f32[64,1024]{1,0:T(8,128)}, f32[64,1024]{1,0:T(8,128)S(1)}, u32[]{:S(2)}, u32[]{:S(2)}) collective-permute-start(f32[64,1024]{1,0:T(8,128)} %bitcast.3), channel_id=1, source_target_pairs={{0,2},{1,3},{2,0},{3,1},{4,6},{5,7},{6,4},{7,5},{8,10},{9,11},{10,... | collective-permute-start | bytes 786440 | tf_op jit(solution)/shard_map/ppermute | solution.py:36
  3.7 8.8 %collective-permute-start = (f32[64,1024]{1,0:T(8,128)}, f32[64,1024]{1,0:T(8,128)S(1)}, u32[]{:S(2)}, u32[]{:S(2)}) collective-permute-start(f32[64,1024]{1,0:T(8,128)} %bitcast.4), channel_id=1, source_target_pairs={{0,1},{1,0},{2,3},{3,2},{4,5},{5,4},{6,7},{7,6},{8,9},{9,8},{10,11... | collective-permute-start | bytes 786440 | tf_op jit(solution)/shard_map/ppermute | solution.py:36
  10.2 5.3 %collective-permute-start.2 = (f32[64,1024]{1,0:T(8,128)S(1)}, f32[64,1024]{1,0:T(8,128)S(1)}, u32[]{:S(2)}, u32[]{:S(2)}) collective-permute-start(f32[64,1024]{1,0:T(8,128)S(1)} %collective-permute-done.1.refs_2_.refs_0_), channel_id=1, source_target_pairs={{0,1},{1,0},{2,3},{3,2},{4,5},{5,4},{6,7},{7,6},{8,9},{9,8},{10,11... | collective-permute-start | bytes 786440 | tf_op jit(solution)/shard_map/ppermute | solution.py:36
  13.1 4.8 %collective-permute-start.3 = (f32[72,384]{1,0:T(8,128)S(1)}, f32[72,384]{1,0:T(8,128)S(1)}, u32[]{:S(2)}, u32[]{:S(2)}) collective-permute-start(f32[72,384]{1,0:T(8,128)S(1)} %broadcast_select_fusion.1), channel_id=1, source_target_pairs={{0,4},{1,9},{2,6},{3,11},{4,0},{5,13},{6,2},{7,15},{8,12},{9,1},{1... | collective-permute-start | bytes 331784 | tf_op jit(solution)/shard_map/ppermute | solution.py:41
  16.1 17.7 %copy-start.1 = (f32[1024,64]{0,1:T(8,128)S(1)}, f32[1024,64]{0,1:T(8,128)}, u32[]{:S(2)}) copy-start(f32[1024,64]{0,1:T(8,128)} %param.6) | copy-start | bytes 786436
  16.2 17.7 %copy-start.2 = (f32[256,256]{1,0:T(8,128)S(1)}, f32[256,256]{1,0:T(8,128)}, u32[]{:S(2)}) copy-start(f32[256,256]{1,0:T(8,128)} %factor_ref.1) | copy-start | bytes 786436
  16.2 4.8 %collective-permute-start.7 = (f32[72,384]{1,0:T(8,128)S(1)}, f32[72,384]{1,0:T(8,128)S(1)}, u32[]{:S(2)}, u32[]{:S(2)}) collective-permute-start(f32[72,384]{1,0:T(8,128)S(1)} %broadcast_select_fusion), channel_id=1, source_target_pairs={{0,4},{1,9},{2,6},{3,11},{4,0},{5,13},{6,2},{7,15},{8,12},{9,1},{1... | collective-permute-start | bytes 331784 | tf_op jit(solution)/shard_map/ppermute | solution.py:41
  18.0 17.7 %copy-start = (f32[1024,384]{1,0:T(8,128)S(1)}, f32[1024,384]{1,0:T(8,128)}, u32[]{:S(2)}) copy-start(f32[1024,384]{1,0:T(8,128)} %acc_ref.1) | copy-start | bytes 4718596
  18.0 17.7 %copy-start.4 = (f32[2,384]{1,0:T(2,128)S(1)}, f32[2,384]{1,0:T(2,128)}, u32[]{:S(2)}) copy-start(f32[2,384]{1,0:T(2,128)} %rows_ref.1) | copy-start | bytes 9220
  18.0 5.7 %collective-permute-start.4 = (f32[72,384]{1,0:T(8,128)S(1)}, f32[72,384]{1,0:T(8,128)S(1)}, u32[]{:S(2)}, u32[]{:S(2)}) collective-permute-start(f32[72,384]{1,0:T(8,128)S(1)} %select_add_fusion.1), channel_id=1, source_target_pairs={{0,8},{1,17},{2,10},{3,19},{4,12},{5,21},{6,14},{7,23},{8,0},{9,25... | collective-permute-start | bytes 331784 | tf_op jit(solution)/shard_map/ppermute | solution.py:41
  21.0 5.3 %collective-permute-start.8 = (f32[72,384]{1,0:T(8,128)S(1)}, f32[72,384]{1,0:T(8,128)S(1)}, u32[]{:S(2)}, u32[]{:S(2)}) collective-permute-start(f32[72,384]{1,0:T(8,128)S(1)} %select_add_fusion), channel_id=1, source_target_pairs={{0,8},{1,17},{2,10},{3,19},{4,12},{5,21},{6,14},{7,23},{8,0},{9,25... | collective-permute-start | bytes 331784 | tf_op jit(solution)/shard_map/ppermute | solution.py:41
  23.8 5.7 %collective-permute-start.5 = (f32[72,384]{1,0:T(8,128)S(1)}, f32[72,384]{1,0:T(8,128)S(1)}, u32[]{:S(2)}, u32[]{:S(2)}) collective-permute-start(f32[72,384]{1,0:T(8,128)S(1)} %add.36), channel_id=1, source_target_pairs={{0,16},{1,5},{2,18},{3,7},{4,20},{5,1},{6,22},{7,3},{8,24},{9,13},... | collective-permute-start | bytes 331784 | tf_op jit(solution)/shard_map/ppermute | solution.py:41
  26.4 5.8 %collective-permute-start.9 = (f32[72,384]{1,0:T(8,128)S(1)}, f32[72,384]{1,0:T(8,128)S(1)}, u32[]{:S(2)}, u32[]{:S(2)}) collective-permute-start(f32[72,384]{1,0:T(8,128)S(1)} %add.39), channel_id=1, source_target_pairs={{0,16},{1,5},{2,18},{3,7},{4,20},{5,1},{6,22},{7,3},{8,24},{9,13},... | collective-permute-start | bytes 331784 | tf_op jit(solution)/shard_map/ppermute | solution.py:41
  29.5 6.2 %collective-permute-start.6 = (f32[72,384]{1,0:T(8,128)S(1)}, f32[72,384]{1,0:T(8,128)S(1)}, u32[]{:S(2)}, u32[]{:S(2)}) collective-permute-start(f32[72,384]{1,0:T(8,128)S(1)} %add.37.refs_0_), channel_id=1, source_target_pairs={{0,4},{1,9},{2,6},{3,11},{4,0},{5,13},{6,2},{7,15},{8,12},{9,1},{1... | collective-permute-start | bytes 331784 | tf_op jit(solution)/shard_map/ppermute | solution.py:41
  32.2 5.5 %collective-permute-start.10 = (f32[72,384]{1,0:T(8,128)S(1)}, f32[72,384]{1,0:T(8,128)S(1)}, u32[]{:S(2)}, u32[]{:S(2)}) collective-permute-start(f32[72,384]{1,0:T(8,128)S(1)} %add.40.refs_2_), channel_id=1, source_target_pairs={{0,4},{1,9},{2,6},{3,11},{4,0},{5,13},{6,2},{7,15},{8,12},{9,1},{1... | collective-permute-start | bytes 331784 | tf_op jit(solution)/shard_map/ppermute | solution.py:41

commit v3 on v2

--- a/solution.py
+++ b/solution.py
@@ -6,10 +6,10 @@
 from jax.sharding import PartitionSpec as P
 
 EXTRA = 8
-ORDERS = lambda b: (b, b[1:] + b[:1])
-BLOCKS = (4, 2)
+LANE = 128
 LOADS = 4
-VMEM = 16777216
+STORES = 4
+VMEM = 16 << 20
 LIMIT = pltpu.CompilerParams(vmem_limit_bytes=VMEM)
 ROWS = ((1,), (0,))
 LANES = ((1,), (1,))
@@ -30,6 +30,12 @@
 
 def thrice(left, right, dims=ROWS):
     return once(left[0], right[0], dims) + (once(left[0], right[1], dims) + once(left[1], right[0], dims))
+
+
+def stacked(left, right, dims=ROWS):
+    count = left[0].shape[0]
+    both = once(jnp.concatenate(left, axis=0), right[0], dims)
+    return both[:count] + (both[count:] + once(left[0], right[1], dims))
 
 
 def swap(value, axis, size, distance):
@@ -58,10 +64,23 @@
 
 
 def put(ref, product, check):
-    half = product.shape[0]
-    ref[:half, :] = product
-    ref[half:, :] = jnp.zeros((EXTRA, ref.shape[1]), jnp.float32)
-    ref[half:, :half] = check
+    half, columns = product.shape
+    for t in range(columns // LANE):
+        ref[t * half : (t + 1) * half, :] = product[:, t * LANE : (t + 1) * LANE]
+    end = columns // LANE * half
+    ref[end:, :] = jnp.zeros((EXTRA, LANE), jnp.float32)
+    ref[end:, :half] = check
+
+
+def packed(half, columns):
+    return jax.ShapeDtypeStruct((columns // LANE * half + EXTRA, LANE), jnp.float32)
+
+
+def take(ref, columns):
+    tiles = columns // LANE
+    half = (ref.shape[0] - EXTRA) // tiles
+    product = jnp.concatenate([ref[t * half : (t + 1) * half, :] for t in range(tiles)], axis=1)
+    return product, ref[tiles * half :, :half]
 
 
 def tall_sums(sums_ref):
@@ -71,7 +90,7 @@
 
 def next_kernel(high_ref, low_ref, sums_ref, *refs):
     panel = high_low(jnp.concatenate([ref[...] for ref in refs[:-1]], axis=0))
-    product = thrice(panel, (high_ref[...], low_ref[...]))
+    product = stacked(panel, (high_ref[...], low_ref[...]))
     put(refs[-1], product, thrice(high_low(tall_sums(sums_ref)), panel, LANES))
 
 
@@ -94,7 +113,7 @@
         band = slice(i * chunk, (i + 1) * chunk)
         part = high_low(load_ref[band, :])
         high_ref[band, :], low_ref[band, :] = part
-        product += thrice((panel[0][:, band], panel[1][:, band]), part)
+        product += stacked((panel[0][:, band], panel[1][:, band]), part)
     put(out_ref, product, check)
 
 
@@ -102,7 +121,7 @@
 
 
 def first_products(trailing, piece, sums):
-    out = jax.ShapeDtypeStruct((piece.shape[0] + EXTRA, trailing.shape[1]), jnp.float32)
+    out = packed(piece.shape[0], trailing.shape[1])
     part = jax.ShapeDtypeStruct(trailing.shape, jnp.bfloat16)
     return pl.pallas_call(
         first_kernel,
@@ -120,7 +139,7 @@
         next_kernel,
         in_specs=[VMEM_SPEC] * (3 + len(pieces)),
         out_specs=VMEM_SPEC,
-        out_shape=jax.ShapeDtypeStruct((half + EXTRA, trailing[0].shape[1]), jnp.float32),
+        out_shape=packed(half, trailing[0].shape[1]),
         compiler_params=LIMIT,
     )(*trailing, sums, *pieces)
 
@@ -165,50 +184,71 @@
 
 
 def apply_kernel(acc_ref, high_ref, low_ref, coeff_ref, rows_ref, sums_ref, *refs):
-    parts, (out_ref, row_ref, col_ref) = refs[:-3], refs[-3:]
-    tall = parts[0].shape[0] - EXTRA
-    upto = tall * len(parts)
-    right = high_low(jnp.concatenate([part[:tall, :] for part in parts], axis=0))
+    parts, (out_ref, row_ref, col_ref), (load_ref, sems) = refs[:-5], refs[-5:-2], refs[-2:]
+    rows, columns = acc_ref.shape
+    chunk = rows // LOADS
+    bands = [pl.ds(i * chunk, chunk) for i in range(LOADS)]
+    loads = [pltpu.make_async_copy(acc_ref.at[band], load_ref.at[band], sems.at[i]) for i, band in enumerate(bands)]
+    for load in loads:
+        load.start()
+    took = [take(part, columns) for part in parts]
+    right = high_low(jnp.concatenate([product for product, _ in took], axis=0))
+    upto = right[0].shape[0]
+    check = jnp.concatenate([check for _, check in took], axis=1)
     left = (high_ref[:, :upto], low_ref[:, :upto])
-    out_ref[...] = acc_ref[...] - thrice(left, right)
-    check = jnp.concatenate([part[tall:, :tall] for part in parts], axis=1)
+    row_ref[...] = rows_ref[...] - thrice(high_low(coeff_ref[:, :upto]), right)[: row_ref.shape[0]]
     col_ref[...] = sums_ref[...] - thrice(high_low(check), left, LANES)[: col_ref.shape[0]]
-
-    @pl.when(pl.program_id(0) == 0)
-    def _():
-        row_ref[...] = rows_ref[...] - thrice(high_low(coeff_ref[:, :upto]), right)[: row_ref.shape[0]]
-
-
-def finish_kernel(acc_ref, left_ref, coeff_ref, rows_ref, sums_ref, part_ref, out_ref, row_ref, col_ref):
-    tall = part_ref.shape[0] - EXTRA
-    high, low = high_low(part_ref[:tall, :])
+    for band, load in zip(bands, loads):
+        some = thrice((high_ref[band, :upto], low_ref[band, :upto]), right)
+        load.wait()
+        out_ref[band, :] = load_ref[band, :] - some
+
+
+def applied(acc, high, low, coeff, row_sums, sums, parts):
+    return pl.pallas_call(
+        apply_kernel,
+        in_specs=[pl.BlockSpec(memory_space=pltpu.HBM)] + [VMEM_SPEC] * (5 + len(parts)),
+        out_specs=[VMEM_SPEC] * 3,
+        out_shape=[jax.ShapeDtypeStruct(a.shape, a.dtype) for a in (acc, row_sums, sums)],
+        scratch_shapes=[pltpu.VMEM(acc.shape, acc.dtype), pltpu.SemaphoreType.DMA((LOADS,))],
+        compiler_params=LIMIT,
+    )(pltpu.with_memory_space_constraint(acc, pltpu.HBM), high, low, coeff, row_sums, sums, *parts)
+
+
+def finish_kernel(acc_ref, left_ref, coeff_ref, rows_ref, sums_ref, part_ref, out_ref, row_ref, col_ref, done_ref, row_done, col_done, sems):
+    rows, columns = acc_ref.shape
+    product, check = take(part_ref, columns)
+    high, low = high_low(product)
     right = jnp.concatenate([high, low, high, low], axis=0)
-    left = left_ref[...]
-    out_ref[...] = acc_ref[...] - once(left, right)
-    high, low = high_low(part_ref[tall:, :tall])
-    col_ref[...] = sums_ref[...] - once(jnp.concatenate([high, low, high, low], axis=1), left, LANES)[: col_ref.shape[0]]
-
-    @pl.when(pl.program_id(0) == 0)
-    def _():
-        size = coeff_ref.shape[1]
-        high, low = high_low(coeff_ref[:, size - tall :])
-        row_ref[...] = rows_ref[...] - once(jnp.concatenate([high, high, low, low], axis=1), right)[: row_ref.shape[0]]
-
-
-def update(kernel, blocks, acc, lefts, coeff, row_sums, sums, parts):
-    rows, _ = acc.shape
-    tall = rows // blocks
-    band = lambda array: pl.BlockSpec((tall, array.shape[1]), lambda i: (i, 0))
-    whole = lambda array: pl.BlockSpec(array.shape, lambda i: (0,) * array.ndim)
-    lanes = pl.BlockSpec((sums.shape[0], tall), lambda i: (0, i))
-    return pl.pallas_call(
-        kernel,
-        grid=(blocks,),
-        in_specs=[band(acc)] + [band(left) for left in lefts] + [whole(coeff), whole(row_sums), lanes] + [whole(part) for part in parts],
-        out_specs=[band(acc), whole(row_sums), lanes],
-        out_shape=[jax.ShapeDtypeStruct(a.shape, a.dtype) for a in (acc, row_sums, sums)],
-        compiler_params=LIMIT,
-    )(acc, *lefts, coeff, row_sums, sums, *parts)
+    chunk = rows // STORES
+    stores = []
+    for i in range(STORES):
+        band = pl.ds(i * chunk, chunk)
+        done_ref[band, :] = acc_ref[band, :] - once(left_ref[band, :], right)
+        stores.append(pltpu.make_async_copy(done_ref.at[band], out_ref.at[band], sems.at[i]))
+        stores[-1].start()
+    high, low = high_low(check)
+    col_done[...] = sums_ref[...] - once(jnp.concatenate([high, low, high, low], axis=1), left_ref[...], LANES)[: col_ref.shape[0]]
+    stores.append(pltpu.make_async_copy(col_done, col_ref, sems.at[STORES]))
+    stores[-1].start()
+    high, low = high_low(coeff_ref[:, coeff_ref.shape[1] - product.shape[0] :])
+    row_done[...] = rows_ref[...] - once(jnp.concatenate([high, high, low, low], axis=1), right)[: row_ref.shape[0]]
+    stores.append(pltpu.make_async_copy(row_done, row_ref, sems.at[STORES + 1]))
+    stores[-1].start()
+    for store in stores:
+        store.wait()
+
+
+def finished(acc, left, coeff, row_sums, sums, part):
+    outs = (acc, row_sums, sums)
+    return pl.pallas_call(
+        finish_kernel,
+        in_specs=[VMEM_SPEC] * 6,
+        out_specs=[pl.BlockSpec(memory_space=pltpu.HBM)] * 3,
+        out_shape=[jax.ShapeDtypeStruct(a.shape, a.dtype) for a in outs],
+        scratch_shapes=[pltpu.VMEM(a.shape, a.dtype) for a in outs] + [pltpu.SemaphoreType.DMA((STORES + 2,))],
+        compiler_params=LIMIT,
+    )(acc, left, coeff, row_sums, sums, part)
 
 
 def near(start, count, n_col):
@@ -233,7 +273,7 @@
     summed = []
     order = []
     for g, pieces in enumerate((mine, others)):
-        ways = list(zip(*ORDERS(bits)))
+        ways = list(zip(bits, bits[1:] + bits[:1]))
         side = jnp.where(col % 2 == 0, row // ways[0][0], row // ways[0][1]) % 2
         if g == 0 and quarter == 1:
             parts = [own]
@@ -251,8 +291,8 @@
     order = jnp.concatenate(order) * width
     late = quarter * width
     high, low, last, coeff = spreads(places, order, factor, mine + others, late)
-    acc, row_sums, sums = update(apply_kernel, BLOCKS[0], trailing, (high, low), coeff, row_sums, sums, summed[:-1])
-    updated, row_checks, sums = update(finish_kernel, BLOCKS[1], acc, (last,), coeff, row_sums, sums, summed[-1:])
+    acc, row_sums, sums = applied(trailing, high, low, coeff, row_sums, sums, summed[:-1])
+    updated, row_checks, sums = finished(acc, last, coeff, row_sums, sums, summed[-1])
     return (updated, sums.T, row_checks)
 
 

time: 39.6 us -> 38.8 us (0.980)
  waiting for transfers between devices: 12.3 us -> 11.9 us
    ppermute x8, waiting for transfers between devices: 5.77 us -> 5.35 us  [swap_mixed(): return lax.ppermute(value, ('row', 'col'), pairs)]
  transfers between devices with their start and end apart: 11 -> 11, of which waited for: 7 -> 6; matrix products, arithmetic and copies ran while one was open for 1% -> 1% of each run, Pallas kernels for 20% -> 20%
where the time goes in v3:
time: 38.8 us; the launch traced here: 38.6 us
  starting transfers between devices  16.5 us (43%)
  waiting for transfers between devices  11.9 us (31%)
  Pallas kernels  9.25 us (24%)
  between operations  0.76 us (2%)
    ppermute x8, starting transfers between devices, swap_mixed(): return lax.ppermute(value, ('row', 'col'), pairs)  13.5 us
    ppermute x3, waiting for transfers between devices, swap(): return lax.ppermute(value, axis, [(i, i ^ distance) for i in range(size)])  6.52 us
    ppermute x8, waiting for transfers between devices, swap_mixed(): return lax.ppermute(value, ('row', 'col'), pairs)  5.35 us
    ppermute x3, starting transfers between devices, swap(): return lax.ppermute(value, axis, [(i, i ^ distance) for i in range(size)])  3.07 us
    pallas_call x1, Pallas kernels, first_products(): pl.pallas_call(first_kernel, in_specs=[pl.BlockSpec(memory_space=pltpu.HB...  2.2 us
    pallas_call x1, Pallas kernels, applied(): pl.pallas_call(apply_kernel, in_specs=[pl.BlockSpec(memory_space=pltpu.HB...  2.19 us
    pallas_call x1, Pallas kernels, spreads(): pl.pallas_call(spread_kernel, in_specs=[pl.BlockSpec(memory_space=pltpu.S...  1.9 us
    pallas_call x3, Pallas kernels, next_products(): pl.pallas_call(next_kernel, in_specs=[VMEM_SPEC] * (3 + len(pieces)), out...  1.53 us
  transfers between devices with their start and end apart: 11, of which 6 were waited for; matrix products, arithmetic and copies ran while one was open for 1% of the time, Pallas kernels for 20%

profile of v3, /device:TPU:0, one launch (start us, length us, event | category | flops | bytes accessed | tf_op | source)
XLA Modules:
  0.0 38.6 jit_solution(5272838457603664735)
XLA Ops:
  0.6 0.0 copy-start.2
  0.6 3.1 %collective-permute-start.1 = (f32[64,1024]{1,0:T(8,128)}, f32[64,1024]{1,0:T(8,128)S(1)}, u32[]{:S(2)}, u32[]{:S(2)}) collective-permute-start(f32[64,1024]{1,0:T(8,128)} %bitcast.3), channel_id=1, source_target_pairs={{0,2},{1,3},{2,0},{3,1},{4,6},{5,7},{6,4},{7,5},{8,10},{9,11},{10,... | collective-permute-start | bytes 786440 | tf_op jit(solution)/shard_map/ppermute | solution.py:42
  3.7 0.0 collective-permute-start
  3.7 6.5 %collective-permute-done.1.refs_2_.refs_0_ = f32[64,1024]{1,0:T(8,128)S(1)} collective-permute-done((f32[64,1024]{1,0:T(8,128)}, f32[64,1024]{1,0:T(8,128)S(1)}, u32[]{:S(2)}, u32[]{:S(2)}) %collective-permute-start.1) | collective-permute-done | bytes 262176 | tf_op jit(solution)/shard_map/ppermute | solution.py:42
  10.2 0.0 collective-permute-start.2
  10.2 2.2 %shard_map.77 = (f32[200,128]{1,0:T(8,128)S(1)}, bf16[1024,384]{1,0:T(8,128)(2,1)S(1)}, bf16[1024,384]{1,0:T(8,128)(2,1)S(1)}) custom-call(f32[1024,384]{1,0:T(8,128)} %acc_ref.1, f32[64,1024]{1,0:T(8,128)} %bitcast.5, f32[2,1024]{1,0:T(2,128)} %bitcast.7), custom_call_target="tpu_custom_call" | custom-call | tf_op jit(solution)/shard_map/pallas_call | solution.py:126
  12.4 0.0 collective-permute-done.refs_1_.refs_0_
  12.4 0.0 copy-done.2
  12.5 0.5 %shard_map.78 = f32[200,128]{1,0:T(8,128)S(1)} custom-call(bf16[1024,384]{1,0:T(8,128)(2,1)S(1)} %get-tuple-element.20.high_ref, bf16[1024,384]{1,0:T(8,128)(2,1)S(1)} %get-tuple-element.21.low_ref, f32[2,1024]{1,0:T(2,128)S(1)} %bitcast.8, f32[64,1024]{1,0:T(8,128)S(1)} %collective-permute-done.refs_1_.refs_0_), custom_call_target="tpu_custom_call" | custom-call | tf_op jit(solution)/shard_map/pallas_call | solution.py:138
  13.0 1.8 %collective-permute-start.3 = (f32[200,128]{1,0:T(8,128)S(1)}, f32[200,128]{1,0:T(8,128)S(1)}, u32[]{:S(2)}, u32[]{:S(2)}) collective-permute-start(f32[200,128]{1,0:T(8,128)S(1)} %broadcast_select_fusion.1), channel_id=1, source_target_pairs={{0,4},{1,9},{2,6},{3,11},{4,0},{5,13},{6,2},{7,15},{8,12},{9,1},{1... | collective-permute-start | bytes 307208 | tf_op jit(solution)/shard_map/ppermute | solution.py:47
  14.8 0.5 %shard_map.79 = f32[200,128]{1,0:T(8,128)S(1)} custom-call(bf16[1024,384]{1,0:T(8,128)(2,1)S(1)} %get-tuple-element.20.high_ref, bf16[1024,384]{1,0:T(8,128)(2,1)S(1)} %get-tuple-element.21.low_ref, f32[2,1024]{1,0:T(2,128)S(1)} %bitcast.9, f32[64,1024]{1,0:T(8,128)S(1)} %collective-permute-done.1.refs_2_.refs_0_), custom_call_target="tpu_custom_call" | custom-call | tf_op jit(solution)/shard_map/pallas_call | solution.py:138
  15.3 0.0 collective-permute-done.2.refs_3_.refs_0_
  15.3 0.5 %shard_map.80 = f32[200,128]{1,0:T(8,128)S(1)} custom-call(bf16[1024,384]{1,0:T(8,128)(2,1)S(1)} %get-tuple-element.20.high_ref, bf16[1024,384]{1,0:T(8,128)(2,1)S(1)} %get-tuple-element.21.low_ref, f32[2,1024]{1,0:T(2,128)S(1)} %bitcast.10, f32[64,1024]{1,0:T(8,128)S(1)} %collective-permute-done.2.refs_3_.refs_0_), custom_call_target="tpu_custom_call" | custom-call | tf_op jit(solution)/shard_map/pallas_call | solution.py:138
  15.8 0.0 copy-start
  15.8 0.0 copy-start.1
  15.8 0.4 collective-permute-start.7
  16.2 1.5 %collective-permute-done.3 = f32[200,128]{1,0:T(8,128)S(1)} collective-permute-done((f32[200,128]{1,0:T(8,128)S(1)}, f32[200,128]{1,0:T(8,128)S(1)}, u32[]{:S(2)}, u32[]{:S(2)}) %collective-permute-start.3) | collective-permute-done | bytes 102432 | tf_op jit(solution)/shard_map/ppermute | solution.py:47
  17.7 0.0 copy-start.3
  17.7 1.9 %collective-permute-start.4 = (f32[200,128]{1,0:T(8,128)S(1)}, f32[200,128]{1,0:T(8,128)S(1)}, u32[]{:S(2)}, u32[]{:S(2)}) collective-permute-start(f32[200,128]{1,0:T(8,128)S(1)} %select_add_fusion.1), channel_id=1, source_target_pairs={{0,8},{1,17},{2,10},{3,19},{4,12},{5,21},{6,14},{7,23},{8,0},{9,25... | collective-permute-start | bytes 307208 | tf_op jit(solution)/shard_map/ppermute | solution.py:47
  19.6 1.0 %collective-permute-done.7 = f32[200,128]{1,0:T(8,128)S(1)} collective-permute-done((f32[200,128]{1,0:T(8,128)S(1)}, f32[200,128]{1,0:T(8,128)S(1)}, u32[]{:S(2)}, u32[]{:S(2)}) %collective-permute-start.7) | collective-permute-done | bytes 102432 | tf_op jit(solution)/shard_map/ppermute | solution.py:47
  20.6 1.6 %collective-permute-start.8 = (f32[200,128]{1,0:T(8,128)S(1)}, f32[200,128]{1,0:T(8,128)S(1)}, u32[]{:S(2)}, u32[]{:S(2)}) collective-permute-start(f32[200,128]{1,0:T(8,128)S(1)} %select_add_fusion), channel_id=1, source_target_pairs={{0,8},{1,17},{2,10},{3,19},{4,12},{5,21},{6,14},{7,23},{8,0},{9,25... | collective-permute-start | bytes 307208 | tf_op jit(solution)/shard_map/ppermute | solution.py:47
  22.2 1.1 %collective-permute-done.4 = f32[200,128]{1,0:T(8,128)S(1)} collective-permute-done((f32[200,128]{1,0:T(8,128)S(1)}, f32[200,128]{1,0:T(8,128)S(1)}, u32[]{:S(2)}, u32[]{:S(2)}) %collective-permute-start.4) | collective-permute-done | bytes 102432 | tf_op jit(solution)/shard_map/ppermute | solution.py:47
  23.3 2.5 %collective-permute-start.5 = (f32[200,128]{1,0:T(8,128)S(1)}, f32[200,128]{1,0:T(8,128)S(1)}, u32[]{:S(2)}, u32[]{:S(2)}) collective-permute-start(f32[200,128]{1,0:T(8,128)S(1)} %add.36), channel_id=1, source_target_pairs={{0,16},{1,5},{2,18},{3,7},{4,20},{5,1},{6,22},{7,3},{8,24},{9,13},... | collective-permute-start | bytes 307208 | tf_op jit(solution)/shard_map/ppermute | solution.py:47
  25.8 0.0 collective-permute-done.8
  25.8 2.1 %collective-permute-start.9 = (f32[200,128]{1,0:T(8,128)S(1)}, f32[200,128]{1,0:T(8,128)S(1)}, u32[]{:S(2)}, u32[]{:S(2)}) collective-permute-start(f32[200,128]{1,0:T(8,128)S(1)} %add.39), channel_id=1, source_target_pairs={{0,16},{1,5},{2,18},{3,7},{4,20},{5,1},{6,22},{7,3},{8,24},{9,13},... | collective-permute-start | bytes 307208 | tf_op jit(solution)/shard_map/ppermute | solution.py:47
  28.0 1.0 %collective-permute-done.5 = f32[200,128]{1,0:T(8,128)S(1)} collective-permute-done((f32[200,128]{1,0:T(8,128)S(1)}, f32[200,128]{1,0:T(8,128)S(1)}, u32[]{:S(2)}, u32[]{:S(2)}) %collective-permute-start.5) | collective-permute-done | bytes 102432 | tf_op jit(solution)/shard_map/ppermute | solution.py:47
  29.0 1.6 %collective-permute-start.6 = (f32[200,128]{1,0:T(8,128)S(1)}, f32[200,128]{1,0:T(8,128)S(1)}, u32[]{:S(2)}, u32[]{:S(2)}) collective-permute-start(f32[200,128]{1,0:T(8,128)S(1)} %add.37.refs_0_), channel_id=1, source_target_pairs={{0,4},{1,9},{2,6},{3,11},{4,0},{5,13},{6,2},{7,15},{8,12},{9,1},{1... | collective-permute-start | bytes 307208 | tf_op jit(solution)/shard_map/ppermute | solution.py:47
  30.6 0.9 %collective-permute-done.9 = f32[200,128]{1,0:T(8,128)S(1)} collective-permute-done((f32[200,128]{1,0:T(8,128)S(1)}, f32[200,128]{1,0:T(8,128)S(1)}, u32[]{:S(2)}, u32[]{:S(2)}) %collective-permute-start.9) | collective-permute-done | bytes 102432 | tf_op jit(solution)/shard_map/ppermute | solution.py:47
  31.5 1.5 %collective-permute-start.10 = (f32[200,128]{1,0:T(8,128)S(1)}, f32[200,128]{1,0:T(8,128)S(1)}, u32[]{:S(2)}, u32[]{:S(2)}) collective-permute-start(f32[200,128]{1,0:T(8,128)S(1)} %add.40.refs_2_), channel_id=1, source_target_pairs={{0,4},{1,9},{2,6},{3,11},{4,0},{5,13},{6,2},{7,15},{8,12},{9,1},{1... | collective-permute-start | bytes 307208 | tf_op jit(solution)/shard_map/ppermute | solution.py:47
  33.0 0.1 add_multiply_fusion.order_ref
  33.1 0.0 copy-done
  33.1 0.0 copy-done.1
  33.1 1.9 %shard_map.76 = (bf16[1024,256]{1,0:T(8,128)(2,1)S(1)}, bf16[1024,256]{1,0:T(8,128)(2,1)S(1)}, bf16[1024,256]{1,0:T(8,128)(2,1)S(1)}, f32[8,256]{1,0:T(8,128)S(1)}) custom-call(s32[4]{0:T(128)S(1)} %xor_multiply_fusion.places_ref, s32[4]{0:T(128)S(1)} %add_multiply_fusion.order_ref, f32[256,256]{1,0:T(8,128)S(1)} %copy-done.1, f32[64,1024]{1,0:T(8,128)S(1)} %bitcast.6, ...), custom_call_target="tpu_custom_call" | custom-call | tf_op jit(solution)/shard_map/pallas_call | solution.py:171
  35.0 0.0 collective-permute-done.6.refs_1_
  35.0 0.0 copy-done.3
  35.0 2.2 %shard_map.81 = (f32[1024,384]{1,0:T(8,128)S(1)}, f32[2,384]{1,0:T(2,128)S(1)}, f32[2,1024]{1,0:T(2,128)S(1)}) custom-call(f32[1024,384]{1,0:T(8,128)} %acc_ref.1, bf16[1024,256]{1,0:T(8,128)(2,1)S(1)} %get-tuple-element.16.high_ref, bf16[1024,256]{1,0:T(8,128)(2,1)S(1)} %get-tuple-element.17.low_ref, f32[8,256]{1,0:T(8,128)S(1)} %get-tuple-element.18.coeff_ref, ...), custom_call_target="tpu_custom_call" | custom-call | tf_op jit(solution)/shard_map/pallas_call | solution.py:208
  37.2 0.0 collective-permute-done.10.part_ref
  37.2 1.4 %shard_map.82 = (f32[1024,384]{1,0:T(8,128)}, f32[2,384]{1,0:T(2,128)}, f32[2,1024]{1,0:T(2,128)}) custom-call(f32[1024,384]{1,0:T(8,128)S(1)} %get-tuple-element.22.acc_ref, bf16[1024,256]{1,0:T(8,128)(2,1)S(1)} %get-tuple-element.23.left_ref, f32[8,256]{1,0:T(8,128)S(1)} %get-tuple-element.18.coeff_ref, f32[2,384]{1,0:T(2,128)S(1)} %get-tuple-element.24.rows_ref, ...), custom_call_target="tpu_custom_call" | custom-call | tf_op jit(solution)/shard_map/pallas_call | solution.py:244
  (10 shorter events, 0.1 us)
Async XLA Ops:
  0.6 11.8 %copy-start.2 = (f32[1024,2]{0,1:T(2,128)S(1)}, f32[1024,2]{0,1:T(2,128)}, u32[]{:S(2)}) copy-start(f32[1024,2]{0,1:T(2,128)} %param.8) | copy-start | bytes 24580
  0.6 9.6 %collective-permute-start.1 = (f32[64,1024]{1,0:T(8,128)}, f32[64,1024]{1,0:T(8,128)S(1)}, u32[]{:S(2)}, u32[]{:S(2)}) collective-permute-start(f32[64,1024]{1,0:T(8,128)} %bitcast.3), channel_id=1, source_target_pairs={{0,2},{1,3},{2,0},{3,1},{4,6},{5,7},{6,4},{7,5},{8,10},{9,11},{10,... | collective-permute-start | bytes 786440 | tf_op jit(solution)/shard_map/ppermute | solution.py:42
  3.7 8.7 %collective-permute-start = (f32[64,1024]{1,0:T(8,128)}, f32[64,1024]{1,0:T(8,128)S(1)}, u32[]{:S(2)}, u32[]{:S(2)}) collective-permute-start(f32[64,1024]{1,0:T(8,128)} %bitcast.4), channel_id=1, source_target_pairs={{0,1},{1,0},{2,3},{3,2},{4,5},{5,4},{6,7},{7,6},{8,9},{9,8},{10,11... | collective-permute-start | bytes 786440 | tf_op jit(solution)/shard_map/ppermute | solution.py:42
  10.2 5.1 %collective-permute-start.2 = (f32[64,1024]{1,0:T(8,128)S(1)}, f32[64,1024]{1,0:T(8,128)S(1)}, u32[]{:S(2)}, u32[]{:S(2)}) collective-permute-start(f32[64,1024]{1,0:T(8,128)S(1)} %collective-permute-done.1.refs_2_.refs_0_), channel_id=1, source_target_pairs={{0,1},{1,0},{2,3},{3,2},{4,5},{5,4},{6,7},{7,6},{8,9},{9,8},{10,11... | collective-permute-start | bytes 786440 | tf_op jit(solution)/shard_map/ppermute | solution.py:42
  13.0 4.7 %collective-permute-start.3 = (f32[200,128]{1,0:T(8,128)S(1)}, f32[200,128]{1,0:T(8,128)S(1)}, u32[]{:S(2)}, u32[]{:S(2)}) collective-permute-start(f32[200,128]{1,0:T(8,128)S(1)} %broadcast_select_fusion.1), channel_id=1, source_target_pairs={{0,4},{1,9},{2,6},{3,11},{4,0},{5,13},{6,2},{7,15},{8,12},{9,1},{1... | collective-permute-start | bytes 307208 | tf_op jit(solution)/shard_map/ppermute | solution.py:47
  15.8 17.3 %copy-start = (f32[1024,64]{0,1:T(8,128)S(1)}, f32[1024,64]{0,1:T(8,128)}, u32[]{:S(2)}) copy-start(f32[1024,64]{0,1:T(8,128)} %param.6) | copy-start | bytes 786436
  15.8 17.3 %copy-start.1 = (f32[256,256]{1,0:T(8,128)S(1)}, f32[256,256]{1,0:T(8,128)}, u32[]{:S(2)}) copy-start(f32[256,256]{1,0:T(8,128)} %factor_ref.1) | copy-start | bytes 786436
  15.8 4.7 %collective-permute-start.7 = (f32[200,128]{1,0:T(8,128)S(1)}, f32[200,128]{1,0:T(8,128)S(1)}, u32[]{:S(2)}, u32[]{:S(2)}) collective-permute-start(f32[200,128]{1,0:T(8,128)S(1)} %broadcast_select_fusion), channel_id=1, source_target_pairs={{0,4},{1,9},{2,6},{3,11},{4,0},{5,13},{6,2},{7,15},{8,12},{9,1},{1... | collective-permute-start | bytes 307208 | tf_op jit(solution)/shard_map/ppermute | solution.py:47
  17.7 17.3 %copy-start.3 = (f32[2,384]{1,0:T(2,128)S(1)}, f32[2,384]{1,0:T(2,128)}, u32[]{:S(2)}) copy-start(f32[2,384]{1,0:T(2,128)} %rows_ref.1) | copy-start | bytes 9220
  17.7 5.6 %collective-permute-start.4 = (f32[200,128]{1,0:T(8,128)S(1)}, f32[200,128]{1,0:T(8,128)S(1)}, u32[]{:S(2)}, u32[]{:S(2)}) collective-permute-start(f32[200,128]{1,0:T(8,128)S(1)} %select_add_fusion.1), channel_id=1, source_target_pairs={{0,8},{1,17},{2,10},{3,19},{4,12},{5,21},{6,14},{7,23},{8,0},{9,25... | collective-permute-start | bytes 307208 | tf_op jit(solution)/shard_map/ppermute | solution.py:47
  20.6 5.2 %collective-permute-start.8 = (f32[200,128]{1,0:T(8,128)S(1)}, f32[200,128]{1,0:T(8,128)S(1)}, u32[]{:S(2)}, u32[]{:S(2)}) collective-permute-start(f32[200,128]{1,0:T(8,128)S(1)} %select_add_fusion), channel_id=1, source_target_pairs={{0,8},{1,17},{2,10},{3,19},{4,12},{5,21},{6,14},{7,23},{8,0},{9,25... | collective-permute-start | bytes 307208 | tf_op jit(solution)/shard_map/ppermute | solution.py:47
  23.3 5.6 %collective-permute-start.5 = (f32[200,128]{1,0:T(8,128)S(1)}, f32[200,128]{1,0:T(8,128)S(1)}, u32[]{:S(2)}, u32[]{:S(2)}) collective-permute-start(f32[200,128]{1,0:T(8,128)S(1)} %add.36), channel_id=1, source_target_pairs={{0,16},{1,5},{2,18},{3,7},{4,20},{5,1},{6,22},{7,3},{8,24},{9,13},... | collective-permute-start | bytes 307208 | tf_op jit(solution)/shard_map/ppermute | solution.py:47
  25.8 5.6 %collective-permute-start.9 = (f32[200,128]{1,0:T(8,128)S(1)}, f32[200,128]{1,0:T(8,128)S(1)}, u32[]{:S(2)}, u32[]{:S(2)}) collective-permute-start(f32[200,128]{1,0:T(8,128)S(1)} %add.39), channel_id=1, source_target_pairs={{0,16},{1,5},{2,18},{3,7},{4,20},{5,1},{6,22},{7,3},{8,24},{9,13},... | collective-permute-start | bytes 307208 | tf_op jit(solution)/shard_map/ppermute | solution.py:47
  29.0 6.0 %collective-permute-start.6 = (f32[200,128]{1,0:T(8,128)S(1)}, f32[200,128]{1,0:T(8,128)S(1)}, u32[]{:S(2)}, u32[]{:S(2)}) collective-permute-start(f32[200,128]{1,0:T(8,128)S(1)} %add.37.refs_0_), channel_id=1, source_target_pairs={{0,4},{1,9},{2,6},{3,11},{4,0},{5,13},{6,2},{7,15},{8,12},{9,1},{1... | collective-permute-start | bytes 307208 | tf_op jit(solution)/shard_map/ppermute | solution.py:47
  31.5 5.7 %collective-permute-start.10 = (f32[200,128]{1,0:T(8,128)S(1)}, f32[200,128]{1,0:T(8,128)S(1)}, u32[]{:S(2)}, u32[]{:S(2)}) collective-permute-start(f32[200,128]{1,0:T(8,128)S(1)} %add.40.refs_2_), channel_id=1, source_target_pairs={{0,4},{1,9},{2,6},{3,11},{4,0},{5,13},{6,2},{7,15},{8,12},{9,1},{1... | collective-permute-start | bytes 307208 | tf_op jit(solution)/shard_map/ppermute | solution.py:47

commit v4 on v3

--- a/solution.py
+++ b/solution.py
@@ -8,7 +8,7 @@
 EXTRA = 8
 LANE = 128
 LOADS = 4
-STORES = 4
+STORES = 8
 VMEM = 16 << 20
 LIMIT = pltpu.CompilerParams(vmem_limit_bytes=VMEM)
 ROWS = ((1,), (0,))
@@ -83,15 +83,14 @@
     return product, ref[tiles * half :, :half]
 
 
-def tall_sums(sums_ref):
-    count, rows = sums_ref.shape
-    return jnp.concatenate([sums_ref[...], jnp.zeros((EXTRA - count, rows), jnp.float32)], axis=0)
-
-
-def next_kernel(high_ref, low_ref, sums_ref, *refs):
+def split_check(product, columns):
+    return product[:, :columns], jnp.transpose(product[:, columns:])[:EXTRA]
+
+
+def next_kernel(high_ref, low_ref, *refs):
     panel = high_low(jnp.concatenate([ref[...] for ref in refs[:-1]], axis=0))
     product = stacked(panel, (high_ref[...], low_ref[...]))
-    put(refs[-1], product, thrice(high_low(tall_sums(sums_ref)), panel, LANES))
+    put(refs[-1], *split_check(product, high_ref.shape[1] - LANE))
 
 
 def first_kernel(trailing_ref, piece_ref, sums_ref, out_ref, high_ref, low_ref, load_ref, panel_ref, check_ref, sems):
@@ -106,15 +105,16 @@
     loads[0].wait()
     loads[1].wait()
     panel = high_low(panel_ref[...])
-    check = thrice(high_low(tall_sums(check_ref)), panel, LANES)
-    product = jnp.zeros((panel[0].shape[0], trailing_ref.shape[1]), jnp.float32)
+    columns = trailing_ref.shape[1]
+    sums = jnp.transpose(jnp.concatenate([check_ref[...], jnp.zeros((LANE - check_ref.shape[0], rows), jnp.float32)], axis=0))
+    high_ref[:, columns:], low_ref[:, columns:] = high_low(sums)
+    product = jnp.zeros((panel[0].shape[0], columns + LANE), jnp.float32)
     for i in range(LOADS):
         loads[2 + i].wait()
         band = slice(i * chunk, (i + 1) * chunk)
-        part = high_low(load_ref[band, :])
-        high_ref[band, :], low_ref[band, :] = part
-        product += stacked((panel[0][:, band], panel[1][:, band]), part)
-    put(out_ref, product, check)
+        high_ref[band, :columns], low_ref[band, :columns] = high_low(load_ref[band, :])
+        product += stacked((panel[0][:, band], panel[1][:, band]), (high_ref[band, :], low_ref[band, :]))
+    put(out_ref, *split_check(product, columns))
 
 
 VMEM_SPEC = pl.BlockSpec(memory_space=pltpu.VMEM)
@@ -122,7 +122,7 @@
 
 def first_products(trailing, piece, sums):
     out = packed(piece.shape[0], trailing.shape[1])
-    part = jax.ShapeDtypeStruct(trailing.shape, jnp.bfloat16)
+    part = jax.ShapeDtypeStruct((trailing.shape[0], trailing.shape[1] + LANE), jnp.bfloat16)
     return pl.pallas_call(
         first_kernel,
         in_specs=[pl.BlockSpec(memory_space=pltpu.HBM)] * 3,
@@ -133,15 +133,15 @@
     )(*[pltpu.with_memory_space_constraint(a, pltpu.HBM) for a in (trailing, piece, sums)])
 
 
-def next_products(trailing, sums, pieces):
+def next_products(trailing, pieces):
     half = sum(piece.shape[0] for piece in pieces)
     return pl.pallas_call(
         next_kernel,
-        in_specs=[VMEM_SPEC] * (3 + len(pieces)),
+        in_specs=[VMEM_SPEC] * (2 + len(pieces)),
         out_specs=VMEM_SPEC,
-        out_shape=packed(half, trailing[0].shape[1]),
-        compiler_params=LIMIT,
-    )(*trailing, sums, *pieces)
+        out_shape=packed(half, trailing[0].shape[1] - LANE),
+        compiler_params=LIMIT,
+    )(*trailing, *pieces)
 
 
 def spread_kernel(places_ref, order_ref, factor_ref, *refs):
@@ -278,8 +278,8 @@
         if g == 0 and quarter == 1:
             parts = [own]
         else:
-            parts = [next_products((high, low), sums, pieces[:quarter])]
-        parts.append(next_products((high, low), sums, pieces[quarter:]))
+            parts = [next_products((high, low), pieces[:quarter])]
+        parts.append(next_products((high, low), pieces[quarter:]))
         total = jnp.where(side == 0, parts[0], parts[1])
         value = jnp.where(side == 0, parts[1], parts[0])
         for way in ways:

time: 38.8 us -> 38.5 us (level)
  no operation moved by 1% of the time
where the time goes in v4:
time: 38.5 us; the launch traced here: 38.3 us
  starting transfers between devices  16.5 us (43%)
  waiting for transfers between devices  11.9 us (31%)
  Pallas kernels  8.95 us (23%)
  between operations  0.73 us (2%)
    ppermute x8, starting transfers between devices, swap_mixed(): return lax.ppermute(value, ('row', 'col'), pairs)  13.5 us
    ppermute x3, waiting for transfers between devices, swap(): return lax.ppermute(value, axis, [(i, i ^ distance) for i in range(size)])  6.52 us
    ppermute x8, waiting for transfers between devices, swap_mixed(): return lax.ppermute(value, ('row', 'col'), pairs)  5.37 us
    ppermute x3, starting transfers between devices, swap(): return lax.ppermute(value, axis, [(i, i ^ distance) for i in range(size)])  3.07 us
    pallas_call x1, Pallas kernels, applied(): pl.pallas_call(apply_kernel, in_specs=[pl.BlockSpec(memory_space=pltpu.HB...  2.18 us
    pallas_call x1, Pallas kernels, first_products(): pl.pallas_call(first_kernel, in_specs=[pl.BlockSpec(memory_space=pltpu.HB...  1.92 us
    pallas_call x1, Pallas kernels, spreads(): pl.pallas_call(spread_kernel, in_specs=[pl.BlockSpec(memory_space=pltpu.S...  1.9 us
    pallas_call x3, Pallas kernels, next_products(): pl.pallas_call(next_kernel, in_specs=[VMEM_SPEC] * (2 + len(pieces)), out...  1.53 us
  transfers between devices with their start and end apart: 11, of which 6 were waited for; matrix products, arithmetic and copies ran while one was open for 1% of the time, Pallas kernels for 20%

profile of v4, /device:TPU:0, one launch (start us, length us, event | category | flops | bytes accessed | tf_op | source)
XLA Modules:
  0.0 38.3 jit_solution(8089164464179649768)
XLA Ops:
  0.6 3.1 %collective-permute-start.1 = (f32[64,1024]{1,0:T(8,128)}, f32[64,1024]{1,0:T(8,128)S(1)}, u32[]{:S(2)}, u32[]{:S(2)}) collective-permute-start(f32[64,1024]{1,0:T(8,128)} %bitcast.3), channel_id=1, source_target_pairs={{0,2},{1,3},{2,0},{3,1},{4,6},{5,7},{6,4},{7,5},{8,10},{9,11},{10,... | collective-permute-start | bytes 786440 | tf_op jit(solution)/shard_map/ppermute | solution.py:42
  3.7 0.0 collective-permute-start
  3.7 6.5 %collective-permute-done.1.refs_2_.refs_0_ = f32[64,1024]{1,0:T(8,128)S(1)} collective-permute-done((f32[64,1024]{1,0:T(8,128)}, f32[64,1024]{1,0:T(8,128)S(1)}, u32[]{:S(2)}, u32[]{:S(2)}) %collective-permute-start.1) | collective-permute-done | bytes 262176 | tf_op jit(solution)/shard_map/ppermute | solution.py:42
  10.2 0.0 collective-permute-start.2
  10.2 1.9 %shard_map.77 = (f32[200,128]{1,0:T(8,128)S(1)}, bf16[1024,512]{1,0:T(8,128)(2,1)S(1)}, bf16[1024,512]{1,0:T(8,128)(2,1)S(1)}) custom-call(f32[1024,384]{1,0:T(8,128)} %acc_ref.1, f32[64,1024]{1,0:T(8,128)} %bitcast.5, f32[2,1024]{1,0:T(2,128)} %bitcast.7), custom_call_target="tpu_custom_call" | custom-call | tf_op jit(solution)/shard_map/pallas_call | solution.py:126
  12.1 0.0 collective-permute-done.refs_1_.refs_0_
  12.2 0.5 %shard_map.78 = f32[200,128]{1,0:T(8,128)S(1)} custom-call(bf16[1024,512]{1,0:T(8,128)(2,1)S(1)} %get-tuple-element.20.high_ref, bf16[1024,512]{1,0:T(8,128)(2,1)S(1)} %get-tuple-element.21.low_ref, f32[64,1024]{1,0:T(8,128)S(1)} %collective-permute-done.refs_1_.refs_0_), custom_call_target="tpu_custom_call" | custom-call | tf_op jit(solution)/shard_map/pallas_call | solution.py:138
  12.7 1.8 %collective-permute-start.3 = (f32[200,128]{1,0:T(8,128)S(1)}, f32[200,128]{1,0:T(8,128)S(1)}, u32[]{:S(2)}, u32[]{:S(2)}) collective-permute-start(f32[200,128]{1,0:T(8,128)S(1)} %broadcast_select_fusion.1), channel_id=1, source_target_pairs={{0,4},{1,9},{2,6},{3,11},{4,0},{5,13},{6,2},{7,15},{8,12},{9,1},{1... | collective-permute-start | bytes 307208 | tf_op jit(solution)/shard_map/ppermute | solution.py:47
  14.5 0.5 %shard_map.79 = f32[200,128]{1,0:T(8,128)S(1)} custom-call(bf16[1024,512]{1,0:T(8,128)(2,1)S(1)} %get-tuple-element.20.high_ref, bf16[1024,512]{1,0:T(8,128)(2,1)S(1)} %get-tuple-element.21.low_ref, f32[64,1024]{1,0:T(8,128)S(1)} %collective-permute-done.1.refs_2_.refs_0_), custom_call_target="tpu_custom_call" | custom-call | tf_op jit(solution)/shard_map/pallas_call | solution.py:138
  15.0 0.0 collective-permute-done.2.refs_3_.refs_0_
  15.0 0.5 %shard_map.80 = f32[200,128]{1,0:T(8,128)S(1)} custom-call(bf16[1024,512]{1,0:T(8,128)(2,1)S(1)} %get-tuple-element.20.high_ref, bf16[1024,512]{1,0:T(8,128)(2,1)S(1)} %get-tuple-element.21.low_ref, f32[64,1024]{1,0:T(8,128)S(1)} %collective-permute-done.2.refs_3_.refs_0_), custom_call_target="tpu_custom_call" | custom-call | tf_op jit(solution)/shard_map/pallas_call | solution.py:138
  15.5 0.0 copy-start
  15.5 0.0 copy-start.1
  15.5 0.4 %collective-permute-start.7 = (f32[200,128]{1,0:T(8,128)S(1)}, f32[200,128]{1,0:T(8,128)S(1)}, u32[]{:S(2)}, u32[]{:S(2)}) collective-permute-start(f32[200,128]{1,0:T(8,128)S(1)} %broadcast_select_fusion), channel_id=1, source_target_pairs={{0,4},{1,9},{2,6},{3,11},{4,0},{5,13},{6,2},{7,15},{8,12},{9,1},{1... | collective-permute-start | bytes 307208 | tf_op jit(solution)/shard_map/ppermute | solution.py:47
  15.9 1.5 %collective-permute-done.3 = f32[200,128]{1,0:T(8,128)S(1)} collective-permute-done((f32[200,128]{1,0:T(8,128)S(1)}, f32[200,128]{1,0:T(8,128)S(1)}, u32[]{:S(2)}, u32[]{:S(2)}) %collective-permute-start.3) | collective-permute-done | bytes 102432 | tf_op jit(solution)/shard_map/ppermute | solution.py:47
  17.4 0.0 copy-start.2
  17.4 0.0 copy-start.3
  17.5 1.9 %collective-permute-start.4 = (f32[200,128]{1,0:T(8,128)S(1)}, f32[200,128]{1,0:T(8,128)S(1)}, u32[]{:S(2)}, u32[]{:S(2)}) collective-permute-start(f32[200,128]{1,0:T(8,128)S(1)} %select_add_fusion.1), channel_id=1, source_target_pairs={{0,8},{1,17},{2,10},{3,19},{4,12},{5,21},{6,14},{7,23},{8,0},{9,25... | collective-permute-start | bytes 307208 | tf_op jit(solution)/shard_map/ppermute | solution.py:47
  19.3 0.9 %collective-permute-done.7 = f32[200,128]{1,0:T(8,128)S(1)} collective-permute-done((f32[200,128]{1,0:T(8,128)S(1)}, f32[200,128]{1,0:T(8,128)S(1)}, u32[]{:S(2)}, u32[]{:S(2)}) %collective-permute-start.7) | collective-permute-done | bytes 102432 | tf_op jit(solution)/shard_map/ppermute | solution.py:47
  20.3 1.6 %collective-permute-start.8 = (f32[200,128]{1,0:T(8,128)S(1)}, f32[200,128]{1,0:T(8,128)S(1)}, u32[]{:S(2)}, u32[]{:S(2)}) collective-permute-start(f32[200,128]{1,0:T(8,128)S(1)} %select_add_fusion), channel_id=1, source_target_pairs={{0,8},{1,17},{2,10},{3,19},{4,12},{5,21},{6,14},{7,23},{8,0},{9,25... | collective-permute-start | bytes 307208 | tf_op jit(solution)/shard_map/ppermute | solution.py:47
  21.9 1.1 %collective-permute-done.4 = f32[200,128]{1,0:T(8,128)S(1)} collective-permute-done((f32[200,128]{1,0:T(8,128)S(1)}, f32[200,128]{1,0:T(8,128)S(1)}, u32[]{:S(2)}, u32[]{:S(2)}) %collective-permute-start.4) | collective-permute-done | bytes 102432 | tf_op jit(solution)/shard_map/ppermute | solution.py:47
  23.0 2.4 %collective-permute-start.5 = (f32[200,128]{1,0:T(8,128)S(1)}, f32[200,128]{1,0:T(8,128)S(1)}, u32[]{:S(2)}, u32[]{:S(2)}) collective-permute-start(f32[200,128]{1,0:T(8,128)S(1)} %add.36), channel_id=1, source_target_pairs={{0,16},{1,5},{2,18},{3,7},{4,20},{5,1},{6,22},{7,3},{8,24},{9,13},... | collective-permute-start | bytes 307208 | tf_op jit(solution)/shard_map/ppermute | solution.py:47
  25.5 0.0 collective-permute-done.8
  25.5 2.2 %collective-permute-start.9 = (f32[200,128]{1,0:T(8,128)S(1)}, f32[200,128]{1,0:T(8,128)S(1)}, u32[]{:S(2)}, u32[]{:S(2)}) collective-permute-start(f32[200,128]{1,0:T(8,128)S(1)} %add.39), channel_id=1, source_target_pairs={{0,16},{1,5},{2,18},{3,7},{4,20},{5,1},{6,22},{7,3},{8,24},{9,13},... | collective-permute-start | bytes 307208 | tf_op jit(solution)/shard_map/ppermute | solution.py:47
  27.7 1.0 %collective-permute-done.5 = f32[200,128]{1,0:T(8,128)S(1)} collective-permute-done((f32[200,128]{1,0:T(8,128)S(1)}, f32[200,128]{1,0:T(8,128)S(1)}, u32[]{:S(2)}, u32[]{:S(2)}) %collective-permute-start.5) | collective-permute-done | bytes 102432 | tf_op jit(solution)/shard_map/ppermute | solution.py:47
  28.7 1.6 %collective-permute-start.6 = (f32[200,128]{1,0:T(8,128)S(1)}, f32[200,128]{1,0:T(8,128)S(1)}, u32[]{:S(2)}, u32[]{:S(2)}) collective-permute-start(f32[200,128]{1,0:T(8,128)S(1)} %add.37.refs_0_), channel_id=1, source_target_pairs={{0,4},{1,9},{2,6},{3,11},{4,0},{5,13},{6,2},{7,15},{8,12},{9,1},{1... | collective-permute-start | bytes 307208 | tf_op jit(solution)/shard_map/ppermute | solution.py:47
  30.3 0.8 %collective-permute-done.9 = f32[200,128]{1,0:T(8,128)S(1)} collective-permute-done((f32[200,128]{1,0:T(8,128)S(1)}, f32[200,128]{1,0:T(8,128)S(1)}, u32[]{:S(2)}, u32[]{:S(2)}) %collective-permute-start.9) | collective-permute-done | bytes 102432 | tf_op jit(solution)/shard_map/ppermute | solution.py:47
  31.2 1.6 %collective-permute-start.10 = (f32[200,128]{1,0:T(8,128)S(1)}, f32[200,128]{1,0:T(8,128)S(1)}, u32[]{:S(2)}, u32[]{:S(2)}) collective-permute-start(f32[200,128]{1,0:T(8,128)S(1)} %add.40.refs_2_), channel_id=1, source_target_pairs={{0,4},{1,9},{2,6},{3,11},{4,0},{5,13},{6,2},{7,15},{8,12},{9,1},{1... | collective-permute-start | bytes 307208 | tf_op jit(solution)/shard_map/ppermute | solution.py:47
  32.7 0.1 add_multiply_fusion.order_ref
  32.8 0.0 copy-done
  32.8 0.0 copy-done.1
  32.8 1.9 %shard_map.76 = (bf16[1024,256]{1,0:T(8,128)(2,1)S(1)}, bf16[1024,256]{1,0:T(8,128)(2,1)S(1)}, bf16[1024,256]{1,0:T(8,128)(2,1)S(1)}, f32[8,256]{1,0:T(8,128)S(1)}) custom-call(s32[4]{0:T(128)S(1)} %xor_multiply_fusion.places_ref, s32[4]{0:T(128)S(1)} %add_multiply_fusion.order_ref, f32[256,256]{1,0:T(8,128)S(1)} %copy-done.1, f32[64,1024]{1,0:T(8,128)S(1)} %bitcast.6, ...), custom_call_target="tpu_custom_call" | custom-call | tf_op jit(solution)/shard_map/pallas_call | solution.py:171
  34.7 0.0 collective-permute-done.6.refs_1_
  34.7 0.0 copy-done.2
  34.7 0.0 copy-done.3
  34.7 2.2 %shard_map.81 = (f32[1024,384]{1,0:T(8,128)S(1)}, f32[2,384]{1,0:T(2,128)S(1)}, f32[2,1024]{1,0:T(2,128)S(1)}) custom-call(f32[1024,384]{1,0:T(8,128)} %acc_ref.1, bf16[1024,256]{1,0:T(8,128)(2,1)S(1)} %get-tuple-element.16.high_ref, bf16[1024,256]{1,0:T(8,128)(2,1)S(1)} %get-tuple-element.17.low_ref, f32[8,256]{1,0:T(8,128)S(1)} %get-tuple-element.18.coeff_ref, ...), custom_call_target="tpu_custom_call" | custom-call | tf_op jit(solution)/shard_map/pallas_call | solution.py:208
  36.9 0.0 collective-permute-done.10.part_ref
  36.9 1.4 %shard_map.82 = (f32[1024,384]{1,0:T(8,128)}, f32[2,384]{1,0:T(2,128)}, f32[2,1024]{1,0:T(2,128)}) custom-call(f32[1024,384]{1,0:T(8,128)S(1)} %get-tuple-element.22.acc_ref, bf16[1024,256]{1,0:T(8,128)(2,1)S(1)} %get-tuple-element.23.left_ref, f32[8,256]{1,0:T(8,128)S(1)} %get-tuple-element.18.coeff_ref, f32[2,384]{1,0:T(2,128)S(1)} %get-tuple-element.24.rows_ref, ...), custom_call_target="tpu_custom_call" | custom-call | tf_op jit(solution)/shard_map/pallas_call | solution.py:244
  (10 shorter events, 0.1 us)
Async XLA Ops:
  0.6 9.6 %collective-permute-start.1 = (f32[64,1024]{1,0:T(8,128)}, f32[64,1024]{1,0:T(8,128)S(1)}, u32[]{:S(2)}, u32[]{:S(2)}) collective-permute-start(f32[64,1024]{1,0:T(8,128)} %bitcast.3), channel_id=1, source_target_pairs={{0,2},{1,3},{2,0},{3,1},{4,6},{5,7},{6,4},{7,5},{8,10},{9,11},{10,... | collective-permute-start | bytes 786440 | tf_op jit(solution)/shard_map/ppermute | solution.py:42
  3.7 8.5 %collective-permute-start = (f32[64,1024]{1,0:T(8,128)}, f32[64,1024]{1,0:T(8,128)S(1)}, u32[]{:S(2)}, u32[]{:S(2)}) collective-permute-start(f32[64,1024]{1,0:T(8,128)} %bitcast.4), channel_id=1, source_target_pairs={{0,1},{1,0},{2,3},{3,2},{4,5},{5,4},{6,7},{7,6},{8,9},{9,8},{10,11... | collective-permute-start | bytes 786440 | tf_op jit(solution)/shard_map/ppermute | solution.py:42
  10.2 4.8 %collective-permute-start.2 = (f32[64,1024]{1,0:T(8,128)S(1)}, f32[64,1024]{1,0:T(8,128)S(1)}, u32[]{:S(2)}, u32[]{:S(2)}) collective-permute-start(f32[64,1024]{1,0:T(8,128)S(1)} %collective-permute-done.1.refs_2_.refs_0_), channel_id=1, source_target_pairs={{0,1},{1,0},{2,3},{3,2},{4,5},{5,4},{6,7},{7,6},{8,9},{9,8},{10,11... | collective-permute-start | bytes 786440 | tf_op jit(solution)/shard_map/ppermute | solution.py:42
  12.7 4.7 %collective-permute-start.3 = (f32[200,128]{1,0:T(8,128)S(1)}, f32[200,128]{1,0:T(8,128)S(1)}, u32[]{:S(2)}, u32[]{:S(2)}) collective-permute-start(f32[200,128]{1,0:T(8,128)S(1)} %broadcast_select_fusion.1), channel_id=1, source_target_pairs={{0,4},{1,9},{2,6},{3,11},{4,0},{5,13},{6,2},{7,15},{8,12},{9,1},{1... | collective-permute-start | bytes 307208 | tf_op jit(solution)/shard_map/ppermute | solution.py:47
  15.5 17.3 %copy-start = (f32[1024,64]{0,1:T(8,128)S(1)}, f32[1024,64]{0,1:T(8,128)}, u32[]{:S(2)}) copy-start(f32[1024,64]{0,1:T(8,128)} %param.6) | copy-start | bytes 786436
  15.5 17.3 %copy-start.1 = (f32[256,256]{1,0:T(8,128)S(1)}, f32[256,256]{1,0:T(8,128)}, u32[]{:S(2)}) copy-start(f32[256,256]{1,0:T(8,128)} %factor_ref.1) | copy-start | bytes 786436
  15.5 4.7 %collective-permute-start.7 = (f32[200,128]{1,0:T(8,128)S(1)}, f32[200,128]{1,0:T(8,128)S(1)}, u32[]{:S(2)}, u32[]{:S(2)}) collective-permute-start(f32[200,128]{1,0:T(8,128)S(1)} %broadcast_select_fusion), channel_id=1, source_target_pairs={{0,4},{1,9},{2,6},{3,11},{4,0},{5,13},{6,2},{7,15},{8,12},{9,1},{1... | collective-permute-start | bytes 307208 | tf_op jit(solution)/shard_map/ppermute | solution.py:47
  17.4 17.3 %copy-start.2 = (f32[1024,2]{0,1:T(2,128)S(1)}, f32[1024,2]{0,1:T(2,128)}, u32[]{:S(2)}) copy-start(f32[1024,2]{0,1:T(2,128)} %param.8) | copy-start | bytes 24580
  17.4 17.3 %copy-start.3 = (f32[2,384]{1,0:T(2,128)S(1)}, f32[2,384]{1,0:T(2,128)}, u32[]{:S(2)}) copy-start(f32[2,384]{1,0:T(2,128)} %rows_ref.1) | copy-start | bytes 9220
  17.5 5.6 %collective-permute-start.4 = (f32[200,128]{1,0:T(8,128)S(1)}, f32[200,128]{1,0:T(8,128)S(1)}, u32[]{:S(2)}, u32[]{:S(2)}) collective-permute-start(f32[200,128]{1,0:T(8,128)S(1)} %select_add_fusion.1), channel_id=1, source_target_pairs={{0,8},{1,17},{2,10},{3,19},{4,12},{5,21},{6,14},{7,23},{8,0},{9,25... | collective-permute-start | bytes 307208 | tf_op jit(solution)/shard_map/ppermute | solution.py:47
  20.3 5.2 %collective-permute-start.8 = (f32[200,128]{1,0:T(8,128)S(1)}, f32[200,128]{1,0:T(8,128)S(1)}, u32[]{:S(2)}, u32[]{:S(2)}) collective-permute-start(f32[200,128]{1,0:T(8,128)S(1)} %select_add_fusion), channel_id=1, source_target_pairs={{0,8},{1,17},{2,10},{3,19},{4,12},{5,21},{6,14},{7,23},{8,0},{9,25... | collective-permute-start | bytes 307208 | tf_op jit(solution)/shard_map/ppermute | solution.py:47
  23.0 5.6 %collective-permute-start.5 = (f32[200,128]{1,0:T(8,128)S(1)}, f32[200,128]{1,0:T(8,128)S(1)}, u32[]{:S(2)}, u32[]{:S(2)}) collective-permute-start(f32[200,128]{1,0:T(8,128)S(1)} %add.36), channel_id=1, source_target_pairs={{0,16},{1,5},{2,18},{3,7},{4,20},{5,1},{6,22},{7,3},{8,24},{9,13},... | collective-permute-start | bytes 307208 | tf_op jit(solution)/shard_map/ppermute | solution.py:47
  25.5 5.6 %collective-permute-start.9 = (f32[200,128]{1,0:T(8,128)S(1)}, f32[200,128]{1,0:T(8,128)S(1)}, u32[]{:S(2)}, u32[]{:S(2)}) collective-permute-start(f32[200,128]{1,0:T(8,128)S(1)} %add.39), channel_id=1, source_target_pairs={{0,16},{1,5},{2,18},{3,7},{4,20},{5,1},{6,22},{7,3},{8,24},{9,13},... | collective-permute-start | bytes 307208 | tf_op jit(solution)/shard_map/ppermute | solution.py:47
  28.7 6.0 %collective-permute-start.6 = (f32[200,128]{1,0:T(8,128)S(1)}, f32[200,128]{1,0:T(8,128)S(1)}, u32[]{:S(2)}, u32[]{:S(2)}) collective-permute-start(f32[200,128]{1,0:T(8,128)S(1)} %add.37.refs_0_), channel_id=1, source_target_pairs={{0,4},{1,9},{2,6},{3,11},{4,0},{5,13},{6,2},{7,15},{8,12},{9,1},{1... | collective-permute-start | bytes 307208 | tf_op jit(solution)/shard_map/ppermute | solution.py:47
  31.2 5.8 %collective-permute-start.10 = (f32[200,128]{1,0:T(8,128)S(1)}, f32[200,128]{1,0:T(8,128)S(1)}, u32[]{:S(2)}, u32[]{:S(2)}) collective-permute-start(f32[200,128]{1,0:T(8,128)S(1)} %add.40.refs_2_), channel_id=1, source_target_pairs={{0,4},{1,9},{2,6},{3,11},{4,0},{5,13},{6,2},{7,15},{8,12},{9,1},{1... | collective-permute-start | bytes 307208 | tf_op jit(solution)/shard_map/ppermute | solution.py:47
